TPU v7x, 768 devices: a whole 4x8x12 slice. The times are simulated.
768 devices in a mesh: gx: 16 (over z_hi, x, core), gy: 48 (over y, z_lo).
Axes of the slice: x: 4, y: 8, z: 12 (z_hi: 2, z_lo: 6; z = z_hi * 6 + z_lo), core: 2. Of those that a mesh axis runs over, the one named last changes fastest.
Arguments:
- adj_electric: float32 [3, 512, 384, 128], P(None, 'gx', 'gy'), may hold values from -6 to 6
- adj_magnetic: float32 [3, 512, 384, 128], P(None, 'gx', 'gy'), may hold values from -6 to 6
- polarization: float32 [3, 512, 384, 128], P(None, 'gx', 'gy'), may hold values from -6 to 6
- pol_rate: float32 [3, 512, 384, 128], P(None, 'gx', 'gy'), may hold values from -6 to 6
- density: float32 [512, 384, 128], P('gx', 'gy'), may hold values from 0 to 1
- forward_rate: float32 [2, 3, 512, 384, 128], P(None, None, 'gx', 'gy'), may hold values from -6 to 6
- design_mask: int32 [512, 384, 128], P('gx', 'gy'), may hold values 0 or 1
- partner_rows: int32 [384], P('gy'), may hold values from 0 to 7, as said below
- filter_radius: int32 [512, 384], P('gx', 'gy'), may hold values from 1 to 4
Outputs:
- electric_out: float32 [3, 512, 384, 128], P(None, 'gx', 'gy')
- magnetic_out: float32 [3, 512, 384, 128], P(None, 'gx', 'gy')
- density_out: float32 [512, 384, 128], P('gx', 'gy')
Inputs may be any that keep to these rules, and one draw needn't show every extreme that they name: `partner_rows`: within each block of 8 rows the values are a permutation of 0 to 7.
All inputs are finite; a program needn't handle non-finite values. No bound on the sum of `design_mask` on one device may be relied on, other than what follows from the above.
Results may differ from a plain program's by a relative error of at most 0.0001.
Values sent between devices are 32-bit elements; how exact they have to be, the bound alone decides.
A program may use at most 32 MiB of HBM per device.

v0:
```python
import math

import jax
import jax.numpy as jnp
from jax import lax
from jax.sharding import PartitionSpec as P

STEPS = 2
RMAX = 4


COURANT = 0.5
DAMPING = 0.9
OMEGA_SQUARED = 0.3
LORENTZ_STRENGTH = 2.0
EPS_MATERIAL = 4.0
UPDATE_STEP = 0.25
SHARPNESS = 4.0
THRESHOLD = 0.5


def padded(array, sides, width):
    for axis, dim in sides:
        peers, length = (lax.axis_size(axis), array.shape[dim])
        up = [(i, (i + 1) % peers) for i in range(peers - 1)]
        down = [(j, i) for i, j in up]
        last = lax.slice_in_dim(array, length - width, length, axis=dim)
        initial = lax.slice_in_dim(array, 0, width, axis=dim)
        before = lax.ppermute(last, axis, up)
        after = lax.ppermute(initial, axis, down)
        array = jnp.concatenate([before, array, after], axis=dim)
    return array


def swapped(block, axis, stride):
    count = lax.axis_size(axis)
    route = []
    for low in range(count):
        high = low | 1 << stride
        if high != low and high < count:
            route += [(low, high), (high, low)]
    return lax.ppermute(block, axis, route)


def ahead(values, dimension):
    count = values.shape[dimension]
    rest = lax.slice_in_dim(values, 1, count, axis=dimension)
    edge = jnp.zeros_like(lax.slice_in_dim(values, 0, 1, axis=dimension))
    return jnp.concatenate([rest, edge], dimension)


def behind(values, dimension):
    count = values.shape[dimension]
    rest = lax.slice_in_dim(values, 0, count - 1, axis=dimension)
    edge = jnp.zeros_like(lax.slice_in_dim(values, 0, 1, axis=dimension))
    return jnp.concatenate([edge, rest], dimension)


def advance(electric, magnetic, polar_now, velocity, material, inside):
    eps_local = 1.0 + (EPS_MATERIAL - 1.0) * material
    e_x, e_y, e_z = (electric[0], electric[1], electric[2])
    curl_e = jnp.stack(
        [
            ahead(e_z, 1) - e_z - (ahead(e_y, 2) - e_y),
            ahead(e_x, 2) - e_x - (ahead(e_z, 0) - e_z),
            ahead(e_y, 0) - e_y - (ahead(e_x, 1) - e_x),
        ]
    )
    magnetic = (magnetic - COURANT * curl_e) * inside
    h_x, h_y, h_z = (magnetic[0], magnetic[1], magnetic[2])
    curl_h = jnp.stack(
        [
            h_z - behind(h_z, 1) - (h_y - behind(h_y, 2)),
            h_x - behind(h_x, 2) - (h_z - behind(h_z, 0)),
            h_y - behind(h_y, 0) - (h_x - behind(h_x, 1)),
        ]
    )
    velocity = (
        DAMPING * velocity
        - OMEGA_SQUARED * polar_now
        + OMEGA_SQUARED * LORENTZ_STRENGTH * material * electric
    )
    polar_now = polar_now + velocity
    electric = (electric + (COURANT * curl_h - velocity) / eps_local) * inside
    return (electric, magnetic, polar_now, velocity)


def project(filtered):
    top = math.tanh(SHARPNESS * THRESHOLD)
    bottom = top + math.tanh(SHARPNESS * (1.0 - THRESHOLD))
    return (top + jnp.tanh(SHARPNESS * (filtered - THRESHOLD))) / bottom


def local(
    adj_electric,
    adj_magnetic,
    polarization,
    pol_rate,
    density,
    forward_rate,
    design_mask,
    partner_rows,
    filter_radius,
):
    rows_x, rows_y, depth = density.shape
    total_x = rows_x * lax.axis_size("gx")
    total_y = rows_y * lax.axis_size("gy")
    x_first = lax.axis_index("gx") * rows_x
    y_first = lax.axis_index("gy") * rows_y

    def inside_frame(width):
        x_cells = x_first + jnp.arange(-width, rows_x + width, dtype=jnp.int32)
        y_cells = y_first + jnp.arange(-width, rows_y + width, dtype=jnp.int32)
        in_x = ((x_cells >= 0) & (x_cells < total_x)).astype(jnp.float32)
        in_y = ((y_cells >= 0) & (y_cells < total_y)).astype(jnp.float32)
        return in_x[:, None, None] * in_y[None, :, None]

    fields = jnp.concatenate([adj_electric, adj_magnetic], 0)
    states = jnp.concatenate([polarization, pol_rate, density[None]], 0)
    framed = padded(jnp.concatenate([fields, states], 0), (("gx", 1), ("gy", 2)), STEPS)
    framed_fields = framed[:6]
    framed_states = framed[6:]
    electric = framed_fields[:3]
    magnetic = framed_fields[3:]
    polar_now = framed_states[:3]
    velocity = framed_states[3:6]
    material = framed_states[6]
    inside = inside_frame(STEPS)
    gradient = jnp.zeros((rows_x, rows_y, depth), jnp.float32)
    for step_index in range(STEPS):
        electric, magnetic, polar_now, velocity = advance(
            electric, magnetic, polar_now, velocity, material, inside
        )
        owned = electric[:, STEPS : STEPS + rows_x, STEPS : STEPS + rows_y, :]
        gradient = gradient + jnp.sum(owned * forward_rate[step_index], axis=0)
    electric_out = electric[:, STEPS : STEPS + rows_x, STEPS : STEPS + rows_y, :]
    magnetic_out = magnetic[:, STEPS : STEPS + rows_x, STEPS : STEPS + rows_y, :]
    partner = gradient
    for bit_index in range(lax.axis_size("gx").bit_length() - 1):
        partner = swapped(partner, "gx", bit_index)
    mirrored = jnp.take(partner[::-1], partner_rows, axis=1)
    symmetric = 0.5 * (gradient + mirrored)
    updated = density - UPDATE_STEP * design_mask.astype(jnp.float32) * symmetric
    width = RMAX - 1
    framed_design = padded(updated, (("gx", 0), ("gy", 1)), width)
    covered = inside_frame(width)
    radius = filter_radius.astype(jnp.float32)[:, :, None]
    numer = jnp.zeros((rows_x, rows_y, depth), jnp.float32)
    denom = jnp.zeros((rows_x, rows_y, 1), jnp.float32)
    for shift_x in range(-width, width + 1):
        for shift_y in range(-width, width + 1):
            distance = math.sqrt(shift_x * shift_x + shift_y * shift_y)
            weight = jnp.maximum(radius - distance, 0.0)
            window = framed_design[
                width + shift_x : width + shift_x + rows_x,
                width + shift_y : width + shift_y + rows_y,
                :,
            ]
            within = covered[
                width + shift_x : width + shift_x + rows_x,
                width + shift_y : width + shift_y + rows_y,
                :,
            ]
            numer = numer + weight * (within * window)
            denom = denom + weight * within
    density_out = project(numer / denom)
    return (electric_out, magnetic_out, density_out)


def solution(mesh):
    in_specs = (
        P(None, "gx", "gy", None),
        P(None, "gx", "gy", None),
        P(None, "gx", "gy", None),
        P(None, "gx", "gy", None),
        P("gx", "gy", None),
        P(None, None, "gx", "gy", None),
        P("gx", "gy", None),
        P("gy"),
        P("gx", "gy"),
    )
    out_specs = (P(None, "gx", "gy", None), P(None, "gx", "gy", None), P("gx", "gy", None))
    return jax.shard_map(local, mesh=mesh, in_specs=in_specs, out_specs=out_specs, check_vma=False)
```

profile of v0, /device:TPU:39, one launch (start us, length us, event | category | flops | bytes accessed | tf_op | source)
XLA Modules:
  0.0 133.9 jit_solution(9960565159963904942)
XLA Ops:
  0.7 1.1 constant_dynamic-update-slice_fusion.3
  1.8 1.0 constant_dynamic-update-slice_fusion.2
  2.9 15.3 %collective-permute-start = (f32[13,2,8,128]{3,2,1,0:T(8,128)S(1)}, f32[13,2,8,128]{3,2,1,0:T(8,128)S(1)}, u32[]{:S(2)}, u32[]{:S(2)}) collective-permute-start(f32[13,2,8,128]{3,2,1,0:T(8,128)S(1)} %get-tuple-element.27), channel_id=1, source_target_pairs={{0,48},{48,96},{96,144},{144,192},{192,240},{240,288},{288,336},{3... | collective-permute-start | bytes 319496 | tf_op jit(solution)/shard_map/ppermute | solution.py:29
  18.3 1.9 %collective-permute-start.1 = (f32[13,2,8,128]{3,2,1,0:T(8,128)S(1)}, f32[13,2,8,128]{3,2,1,0:T(8,128)S(1)}, u32[]{:S(2)}, u32[]{:S(2)}) collective-permute-start(f32[13,2,8,128]{3,2,1,0:T(8,128)S(1)} %get-tuple-element.28), channel_id=1, source_target_pairs={{48,0},{96,48},{144,96},{192,144},{240,192},{288,240},{336,288},{3... | collective-permute-start | bytes 319496 | tf_op jit(solution)/shard_map/ppermute | solution.py:30
  20.3 13.5 %collective-permute-done.1 = f32[13,2,8,128]{3,2,1,0:T(8,128)S(1)} collective-permute-done((f32[13,2,8,128]{3,2,1,0:T(8,128)S(1)}, f32[13,2,8,128]{3,2,1,0:T(8,128)S(1)}, u32[]{:S(2)}, u32[]{:S(2)}) %collective-permute-start.1) | collective-permute-done | bytes 106528 | tf_op jit(solution)/shard_map/ppermute | solution.py:30
  34.2 9.2 %collective-permute-start.2 = (f32[13,36,2,128]{3,2,1,0:T(2,128)S(1)}, f32[13,36,2,128]{3,2,1,0:T(2,128)S(1)}, u32[]{:S(2)}, u32[]{:S(2)}) collective-permute-start(f32[13,36,2,128]{3,2,1,0:T(2,128)S(1)} %get-tuple-element.25), channel_id=1, source_target_pairs={{0,1},{1,2},{2,3},{3,4},{4,5},{5,6},{6,7},{7,8},{8,9},{9,10},{10,1... | collective-permute-start | bytes 1437704 | tf_op jit(solution)/shard_map/ppermute | solution.py:29
  43.4 3.0 %collective-permute-start.3 = (f32[13,36,2,128]{3,2,1,0:T(2,128)S(1)}, f32[13,36,2,128]{3,2,1,0:T(2,128)S(1)}, u32[]{:S(2)}, u32[]{:S(2)}) collective-permute-start(f32[13,36,2,128]{3,2,1,0:T(2,128)S(1)} %get-tuple-element.26), channel_id=1, source_target_pairs={{1,0},{2,1},{3,2},{4,3},{5,4},{6,5},{7,6},{8,7},{9,8},{10,9},{11,1... | collective-permute-start | bytes 1437704 | tf_op jit(solution)/shard_map/ppermute | solution.py:30
  46.6 4.0 %collective-permute-done.2 = f32[13,36,2,128]{3,2,1,0:T(2,128)S(1)} collective-permute-done((f32[13,36,2,128]{3,2,1,0:T(2,128)S(1)}, f32[13,36,2,128]{3,2,1,0:T(2,128)S(1)}, u32[]{:S(2)}, u32[]{:S(2)}) %collective-permute-start.2) | collective-permute-done | bytes 479264 | tf_op jit(solution)/shard_map/ppermute | solution.py:29
  50.6 3.5 %collective-permute-done.3 = f32[13,36,2,128]{3,2,1,0:T(2,128)S(1)} collective-permute-done((f32[13,36,2,128]{3,2,1,0:T(2,128)S(1)}, f32[13,36,2,128]{3,2,1,0:T(2,128)S(1)}, u32[]{:S(2)}, u32[]{:S(2)}) %collective-permute-start.3) | collective-permute-done | bytes 479264 | tf_op jit(solution)/shard_map/ppermute | solution.py:30
  59.4 1.1 fusion.17
  60.6 1.9 %collective-permute-start.4 = (f32[32,8,128]{2,0,1:T(8,128)S(1)}, f32[32,8,128]{2,0,1:T(8,128)S(1)}, u32[]{:S(2)}, u32[]{:S(2)}) collective-permute-start(f32[32,8,128]{2,0,1:T(8,128)S(1)} %copy_add_fusion), channel_id=1, source_target_pairs={{0,48},{48,0},{96,144},{144,96},{192,240},{240,192},{288,336},{336... | collective-permute-start | bytes 393224 | tf_op jit(solution)/shard_map/ppermute | solution.py:42
  62.6 1.2 collective-permute-done.4
  63.8 1.9 %collective-permute-start.5 = (f32[32,8,128]{2,0,1:T(8,128)S(1)}, f32[32,8,128]{2,0,1:T(8,128)S(1)}, u32[]{:S(2)}, u32[]{:S(2)}) collective-permute-start(f32[32,8,128]{2,0,1:T(8,128)S(1)} %collective-permute-done.4), channel_id=1, source_target_pairs={{0,96},{96,0},{48,144},{144,48},{192,288},{288,192},{240,336},{336... | collective-permute-start | bytes 393224 | tf_op jit(solution)/shard_map/ppermute | solution.py:42
  65.8 4.8 %collective-permute-done.5 = f32[32,8,128]{2,0,1:T(8,128)S(1)} collective-permute-done((f32[32,8,128]{2,0,1:T(8,128)S(1)}, f32[32,8,128]{2,0,1:T(8,128)S(1)}, u32[]{:S(2)}, u32[]{:S(2)}) %collective-permute-start.5) | collective-permute-done | bytes 131104 | tf_op jit(solution)/shard_map/ppermute | solution.py:42
  70.6 1.9 %collective-permute-start.6 = (f32[32,8,128]{2,0,1:T(8,128)S(1)}, f32[32,8,128]{2,0,1:T(8,128)S(1)}, u32[]{:S(2)}, u32[]{:S(2)}) collective-permute-start(f32[32,8,128]{2,0,1:T(8,128)S(1)} %collective-permute-done.5), channel_id=1, source_target_pairs={{0,192},{192,0},{48,240},{240,48},{96,288},{288,96},{144,336},{336... | collective-permute-start | bytes 393224 | tf_op jit(solution)/shard_map/ppermute | solution.py:42
  72.6 5.3 %collective-permute-done.6 = f32[32,8,128]{2,0,1:T(8,128)S(1)} collective-permute-done((f32[32,8,128]{2,0,1:T(8,128)S(1)}, f32[32,8,128]{2,0,1:T(8,128)S(1)}, u32[]{:S(2)}, u32[]{:S(2)}) %collective-permute-start.6) | collective-permute-done | bytes 131104 | tf_op jit(solution)/shard_map/ppermute | solution.py:42
  77.8 3.2 %collective-permute-start.7 = (f32[32,8,128]{2,0,1:T(8,128)S(1)}, f32[32,8,128]{2,0,1:T(8,128)S(1)}, u32[]{:S(2)}, u32[]{:S(2)}) collective-permute-start(f32[32,8,128]{2,0,1:T(8,128)S(1)} %collective-permute-done.6), channel_id=1, source_target_pairs={{0,384},{384,0},{48,432},{432,48},{96,480},{480,96},{144,528},{528... | collective-permute-start | bytes 393224 | tf_op jit(solution)/shard_map/ppermute | solution.py:42
  81.0 10.1 %collective-permute-done.7 = f32[32,8,128]{2,0,1:T(8,128)S(1)} collective-permute-done((f32[32,8,128]{2,0,1:T(8,128)S(1)}, f32[32,8,128]{2,0,1:T(8,128)S(1)}, u32[]{:S(2)}, u32[]{:S(2)}) %collective-permute-start.7) | collective-permute-done | bytes 131104 | tf_op jit(solution)/shard_map/ppermute | solution.py:42
  91.8 11.6 %collective-permute-start.8 = (f32[3,8,128]{2,0,1:T(4,128)S(1)}, f32[3,8,128]{2,0,1:T(4,128)S(1)}, u32[]{:S(2)}, u32[]{:S(2)}) collective-permute-start(f32[3,8,128]{2,0,1:T(4,128)S(1)} %get-tuple-element.59), channel_id=1, source_target_pairs={{0,48},{48,96},{96,144},{144,192},{192,240},{240,288},{288,336},{3... | collective-permute-start | bytes 36872 | tf_op jit(solution)/shard_map/ppermute | solution.py:29
  103.5 1.9 %collective-permute-start.9 = (f32[3,8,128]{2,0,1:T(4,128)S(1)}, f32[3,8,128]{2,0,1:T(4,128)S(1)}, u32[]{:S(2)}, u32[]{:S(2)}) collective-permute-start(f32[3,8,128]{2,0,1:T(4,128)S(1)} %get-tuple-element.60), channel_id=1, source_target_pairs={{48,0},{96,48},{144,96},{192,144},{240,192},{288,240},{336,288},{3... | collective-permute-start | bytes 36872 | tf_op jit(solution)/shard_map/ppermute | solution.py:30
  105.4 11.5 %collective-permute-done.9 = f32[3,8,128]{2,0,1:T(4,128)S(1)} collective-permute-done((f32[3,8,128]{2,0,1:T(4,128)S(1)}, f32[3,8,128]{2,0,1:T(4,128)S(1)}, u32[]{:S(2)}, u32[]{:S(2)}) %collective-permute-start.9) | collective-permute-done | bytes 12320 | tf_op jit(solution)/shard_map/ppermute | solution.py:30
  117.0 1.9 %collective-permute-start.10 = (f32[38,3,128]{2,0,1:T(8,128)S(1)}, f32[38,3,128]{2,0,1:T(8,128)S(1)}, u32[]{:S(2)}, u32[]{:S(2)}) collective-permute-start(f32[38,3,128]{2,0,1:T(8,128)S(1)} %get-tuple-element.57), channel_id=1, source_target_pairs={{0,1},{1,2},{2,3},{3,4},{4,5},{5,6},{6,7},{7,8},{8,9},{9,10},{10,1... | collective-permute-start | bytes 175112 | tf_op jit(solution)/shard_map/ppermute | solution.py:29
  118.9 10.3 %collective-permute-start.11 = (f32[38,3,128]{2,0,1:T(8,128)S(1)}, f32[38,3,128]{2,0,1:T(8,128)S(1)}, u32[]{:S(2)}, u32[]{:S(2)}) collective-permute-start(f32[38,3,128]{2,0,1:T(8,128)S(1)} %get-tuple-element.58), channel_id=1, source_target_pairs={{1,0},{2,1},{3,2},{4,3},{5,4},{6,5},{7,6},{8,7},{9,8},{10,9},{11,1... | collective-permute-start | bytes 175112 | tf_op jit(solution)/shard_map/ppermute | solution.py:30
  130.5 2.6 %add_multiply_fusion.1 = f32[32,8,128]{2,0,1:T(8,128)S(1)} fusion(f32[38,11,128]{2,0,1:T(8,128)S(1)} %get-tuple-element.56, f32[3,8,128]{2,0,1:T(4,128)S(1)} %collective-permute-done.9, f32[32,8,128]{2,0,1:T(8,128)S(1)} %fusion.128, f32[38,11,128]{2,0,1:T(8,128)S(1)} %get-tuple-element.55, f32[3,8,128]{2,0,1:T(4,128)S(1)} %collective-permute-done.8, ...), kind=kLoop, calls=%fused_computation.240 | loop fusion | flops 5144576 | bytes 5853184 | tf_op jit(solution)/shard_map/div | solution.py:91
  (76 shorter events, 8.8 us)
Async XLA Ops:
  0.6 2.2 %copy-start.2 = (f32[3,32,8,128]{3,2,1,0:T(8,128)S(1)}, f32[3,32,8,128]{3,2,1,0:T(8,128)}, u32[]{:S(2)}) copy-start(f32[3,32,8,128]{3,2,1,0:T(8,128)} %param.11) | copy-start | bytes 1179652
  0.6 2.2 %copy-start.3 = (f32[3,32,8,128]{3,2,1,0:T(8,128)S(1)}, f32[3,32,8,128]{3,2,1,0:T(8,128)}, u32[]{:S(2)}) copy-start(f32[3,32,8,128]{3,2,1,0:T(8,128)} %param.12) | copy-start | bytes 1179652
  0.7 2.2 %copy-start.1 = (f32[32,8,128]{2,1,0:T(8,128)S(1)}, f32[32,8,128]{2,1,0:T(8,128)}, u32[]{:S(2)}) copy-start(f32[32,8,128]{2,1,0:T(8,128)} %param.13) | copy-start | bytes 393220
  2.9 17.4 %collective-permute-start = (f32[13,2,8,128]{3,2,1,0:T(8,128)S(1)}, f32[13,2,8,128]{3,2,1,0:T(8,128)S(1)}, u32[]{:S(2)}, u32[]{:S(2)}) collective-permute-start(f32[13,2,8,128]{3,2,1,0:T(8,128)S(1)} %get-tuple-element.27), channel_id=1, source_target_pairs={{0,48},{48,96},{96,144},{144,192},{192,240},{240,288},{288,336},{3... | collective-permute-start | bytes 319496 | tf_op jit(solution)/shard_map/ppermute | solution.py:29
  18.3 15.6 %collective-permute-start.1 = (f32[13,2,8,128]{3,2,1,0:T(8,128)S(1)}, f32[13,2,8,128]{3,2,1,0:T(8,128)S(1)}, u32[]{:S(2)}, u32[]{:S(2)}) collective-permute-start(f32[13,2,8,128]{3,2,1,0:T(8,128)S(1)} %get-tuple-element.28), channel_id=1, source_target_pairs={{48,0},{96,48},{144,96},{192,144},{240,192},{288,240},{336,288},{3... | collective-permute-start | bytes 319496 | tf_op jit(solution)/shard_map/ppermute | solution.py:30
  34.2 16.5 %collective-permute-start.2 = (f32[13,36,2,128]{3,2,1,0:T(2,128)S(1)}, f32[13,36,2,128]{3,2,1,0:T(2,128)S(1)}, u32[]{:S(2)}, u32[]{:S(2)}) collective-permute-start(f32[13,36,2,128]{3,2,1,0:T(2,128)S(1)} %get-tuple-element.25), channel_id=1, source_target_pairs={{0,1},{1,2},{2,3},{3,4},{4,5},{5,6},{6,7},{7,8},{8,9},{9,10},{10,1... | collective-permute-start | bytes 1437704 | tf_op jit(solution)/shard_map/ppermute | solution.py:29
  43.4 10.8 %collective-permute-start.3 = (f32[13,36,2,128]{3,2,1,0:T(2,128)S(1)}, f32[13,36,2,128]{3,2,1,0:T(2,128)S(1)}, u32[]{:S(2)}, u32[]{:S(2)}) collective-permute-start(f32[13,36,2,128]{3,2,1,0:T(2,128)S(1)} %get-tuple-element.26), channel_id=1, source_target_pairs={{1,0},{2,1},{3,2},{4,3},{5,4},{6,5},{7,6},{8,7},{9,8},{10,9},{11,1... | collective-permute-start | bytes 1437704 | tf_op jit(solution)/shard_map/ppermute | solution.py:30
  58.3 1.1 copy-start
  59.4 13.1 %copy-start.6 = (s32[8]{0:T(128)S(1)}, s32[8]{0:T(128)}, u32[]{:S(2)}) copy-start(s32[8]{0:T(128)} %param.16) | copy-start | bytes 100
  59.4 32.3 %copy-start.4 = (s32[32,8,128]{2,1,0:T(8,128)S(1)}, s32[32,8,128]{2,1,0:T(8,128)}, u32[]{:S(2)}) copy-start(s32[32,8,128]{2,1,0:T(8,128)} %param.15) | copy-start | bytes 393220
  60.5 44.8 %copy-start.5 = (s32[32,8]{0,1:T(8,128)S(1)}, s32[32,8]{0,1:T(8,128)}, u32[]{:S(2)}) copy-start(s32[32,8]{0,1:T(8,128)} %param.17) | copy-start | bytes 3076
  60.6 3.2 %collective-permute-start.4 = (f32[32,8,128]{2,0,1:T(8,128)S(1)}, f32[32,8,128]{2,0,1:T(8,128)S(1)}, u32[]{:S(2)}, u32[]{:S(2)}) collective-permute-start(f32[32,8,128]{2,0,1:T(8,128)S(1)} %copy_add_fusion), channel_id=1, source_target_pairs={{0,48},{48,0},{96,144},{144,96},{192,240},{240,192},{288,336},{336... | collective-permute-start | bytes 393224 | tf_op jit(solution)/shard_map/ppermute | solution.py:42
  63.8 6.8 %collective-permute-start.5 = (f32[32,8,128]{2,0,1:T(8,128)S(1)}, f32[32,8,128]{2,0,1:T(8,128)S(1)}, u32[]{:S(2)}, u32[]{:S(2)}) collective-permute-start(f32[32,8,128]{2,0,1:T(8,128)S(1)} %collective-permute-done.4), channel_id=1, source_target_pairs={{0,96},{96,0},{48,144},{144,48},{192,288},{288,192},{240,336},{336... | collective-permute-start | bytes 393224 | tf_op jit(solution)/shard_map/ppermute | solution.py:42
  70.6 7.2 %collective-permute-start.6 = (f32[32,8,128]{2,0,1:T(8,128)S(1)}, f32[32,8,128]{2,0,1:T(8,128)S(1)}, u32[]{:S(2)}, u32[]{:S(2)}) collective-permute-start(f32[32,8,128]{2,0,1:T(8,128)S(1)} %collective-permute-done.5), channel_id=1, source_target_pairs={{0,192},{192,0},{48,240},{240,48},{96,288},{288,96},{144,336},{336... | collective-permute-start | bytes 393224 | tf_op jit(solution)/shard_map/ppermute | solution.py:42
  77.8 13.3 %collective-permute-start.7 = (f32[32,8,128]{2,0,1:T(8,128)S(1)}, f32[32,8,128]{2,0,1:T(8,128)S(1)}, u32[]{:S(2)}, u32[]{:S(2)}) collective-permute-start(f32[32,8,128]{2,0,1:T(8,128)S(1)} %collective-permute-done.6), channel_id=1, source_target_pairs={{0,384},{384,0},{48,432},{432,48},{96,480},{480,96},{144,528},{528... | collective-permute-start | bytes 393224 | tf_op jit(solution)/shard_map/ppermute | solution.py:42
  91.8 13.6 %collective-permute-start.8 = (f32[3,8,128]{2,0,1:T(4,128)S(1)}, f32[3,8,128]{2,0,1:T(4,128)S(1)}, u32[]{:S(2)}, u32[]{:S(2)}) collective-permute-start(f32[3,8,128]{2,0,1:T(4,128)S(1)} %get-tuple-element.59), channel_id=1, source_target_pairs={{0,48},{48,96},{96,144},{144,192},{192,240},{240,288},{288,336},{3... | collective-permute-start | bytes 36872 | tf_op jit(solution)/shard_map/ppermute | solution.py:29
  103.5 13.5 %collective-permute-start.9 = (f32[3,8,128]{2,0,1:T(4,128)S(1)}, f32[3,8,128]{2,0,1:T(4,128)S(1)}, u32[]{:S(2)}, u32[]{:S(2)}) collective-permute-start(f32[3,8,128]{2,0,1:T(4,128)S(1)} %get-tuple-element.60), channel_id=1, source_target_pairs={{48,0},{96,48},{144,96},{192,144},{240,192},{288,240},{336,288},{3... | collective-permute-start | bytes 36872 | tf_op jit(solution)/shard_map/ppermute | solution.py:30
  117.0 13.1 %collective-permute-start.10 = (f32[38,3,128]{2,0,1:T(8,128)S(1)}, f32[38,3,128]{2,0,1:T(8,128)S(1)}, u32[]{:S(2)}, u32[]{:S(2)}) collective-permute-start(f32[38,3,128]{2,0,1:T(8,128)S(1)} %get-tuple-element.57), channel_id=1, source_target_pairs={{0,1},{1,2},{2,3},{3,4},{4,5},{5,6},{6,7},{7,8},{8,9},{9,10},{10,1... | collective-permute-start | bytes 175112 | tf_op jit(solution)/shard_map/ppermute | solution.py:29
  118.9 11.6 %collective-permute-start.11 = (f32[38,3,128]{2,0,1:T(8,128)S(1)}, f32[38,3,128]{2,0,1:T(8,128)S(1)}, u32[]{:S(2)}, u32[]{:S(2)}) collective-permute-start(f32[38,3,128]{2,0,1:T(8,128)S(1)} %get-tuple-element.58), channel_id=1, source_target_pairs={{1,0},{2,1},{3,2},{4,3},{5,4},{6,5},{7,6},{8,7},{9,8},{10,9},{11,1... | collective-permute-start | bytes 175112 | tf_op jit(solution)/shard_map/ppermute | solution.py:30
where the time goes:
time: 134 us
  starting transfers between devices  64.1 us (48%)
  waiting for transfers between devices  54.3 us (41%)
  other arithmetic  7.89 us (6%)
  local copies, waits for them, and re-layouts  6.42 us (5%)
    ppermute x4, starting transfers between devices, padded(): before = lax.ppermute(last, axis, up)  38 us
    ppermute x4, waiting for transfers between devices, padded(): after = lax.ppermute(initial, axis, down)  28.9 us
    ppermute x4, waiting for transfers between devices, swapped(): return lax.ppermute(block, axis, route)  21.4 us
    ppermute x4, starting transfers between devices, padded(): after = lax.ppermute(initial, axis, down)  17.1 us
    ppermute x4, starting transfers between devices, swapped(): return lax.ppermute(block, axis, route)  8.89 us
    ppermute x4, waiting for transfers between devices, padded(): before = lax.ppermute(last, axis, up)  4.01 us
    unnamed x19, local copies, waits for them, and re-layouts  3.74 us
  transfers between devices with their start and end apart: 12, of which 9 were waited for; matrix products, arithmetic and copies ran while one was open for 1% of the time, Pallas kernels for 0%

commit v1 on v0

v1 whole, which is shorter than its diff:
```python
import functools
import math

import jax
import jax.numpy as jnp
from jax import lax
from jax.experimental import pallas as pl
from jax.experimental.pallas import tpu as pltpu
from jax.sharding import PartitionSpec as P

STEPS = 2
RMAX = 4
COURANT = 0.5
DAMPING = 0.9
OMEGA_SQUARED = 0.3
LORENTZ_STRENGTH = 2.0
EPS_MATERIAL = 4.0
UPDATE_STEP = 0.25
SHARPNESS = 4.0
THRESHOLD = 0.5

MESH = pl.DeviceIdType.MESH
WIDTH = RMAX - 1
EDGE = 8
ORDER = (0, 2, 1)
SIDES = tuple((i, j) for i in (-1, 0, 1) for j in (-1, 0, 1) if (i, j) != (0, 0))


def kernel(
    nx,
    ny,
    electric_in,
    magnetic_in,
    polar_in,
    rate_in,
    density_in,
    forward_in,
    mask_in,
    partner_in,
    radius_in,
    electric_out,
    magnetic_out,
    density_out,
    v_electric,
    v_magnetic,
    v_polar,
    v_rate,
    v_density,
    v_forward,
    v_mask,
    v_radius,
    efield,
    hfield,
    polar,
    rate,
    inv_eps,
    gradient,
    g_send,
    g_recv,
    g_flip,
    updated,
    covered,
    sums,
    weight_radius,
    inv_denom,
    ye_recv,
    yh_send,
    yh_recv,
    xe_send,
    xe_recv,
    xh_send,
    xh_recv,
    d1_recv,
    d2_recv,
    xf_send,
    xf_recv,
    yf_send,
    yf_recv,
    cf_recv,
    o_electric,
    o_magnetic,
    o_density,
    in_sems,
    out_sems,
    send_sems,
    recv_sems,
):
    rows_x, rows_y = v_radius.shape
    slab = rows_x + 2 * EDGE

    def rows(y, first=EDGE, count=rows_x):
        return pl.ds(y * slab + first, count)

    def own(y):
        start = y * slab + EDGE
        return pl.ds(start if isinstance(start, int) else pl.multiple_of(start, EDGE), rows_x)

    def edge(y, first):
        start = y * slab + first
        return pl.ds(start if isinstance(start, int) else pl.multiple_of(start, EDGE), EDGE)

    gx, gy = lax.axis_index("gx"), lax.axis_index("gy")
    has = {}
    for i, j in SIDES:
        parts = []
        if i:
            parts.append(gx > 0 if i < 0 else gx < nx - 1)
        if j:
            parts.append(gy > 0 if j < 0 else gy < ny - 1)
        has[i, j] = functools.reduce(jnp.logical_and, parts)

    def device(i, j):
        return (lax.rem(gx + i + nx, nx), lax.rem(gy + j + ny, ny))

    mirror = (nx - 1 - gx, gy)

    loads = [
        pltpu.make_async_copy(src, dst, in_sems.at[k])
        for k, (src, dst) in enumerate(
            [
                (electric_in, v_electric),
                (magnetic_in, v_magnetic),
                (polar_in, v_polar),
                (rate_in, v_rate),
                (density_in, v_density),
                (forward_in, v_forward),
                (mask_in, v_mask),
                (radius_in, v_radius),
            ]
        )
    ]
    for load in loads:
        load.start()

    barrier = pltpu.get_barrier_semaphore()
    greeted = jnp.int32(1)
    for side in SIDES:
        greeted = greeted + has[side].astype(jnp.int32)

        @pl.when(has[side])
        def _():
            pl.semaphore_signal(barrier, inc=1, device_id=device(*side), device_id_type=MESH)

    pl.semaphore_signal(barrier, inc=1, device_id=mirror, device_id_type=MESH)

    lane = lax.broadcasted_iota(jnp.int32, (rows_x, 128), 1)

    def ahead_z(v):
        return jnp.where(lane < 127, pltpu.roll(v, 127, 1), 0.0)

    def behind_z(v):
        return jnp.where(lane > 0, pltpu.roll(v, 1, 1), 0.0)

    def over_rows(body, count=rows_y):
        def step(y, carry):
            body(y)
            return carry

        lax.fori_loop(0, count, step, 0)

    zeros_slab = jnp.zeros((rows_x, 128), jnp.float32)
    zeros_edge = jnp.zeros((EDGE, 128), jnp.float32)
    for s in range(STEPS):
        for c in range(3):
            efield[s, c, own(rows_y), :] = zeros_slab

            def clear(y, s=s, c=c):
                efield[s, c, edge(y, EDGE + rows_x), :] = zeros_edge

            over_rows(clear)

    for s in range(STEPS):
        for refs, shape, side in (
            (ye_recv, zeros_slab, (0, 1)),
            (yh_recv, zeros_slab, (0, -1)),
            (xe_recv, zeros_edge, (1, 0)),
            (xh_recv, zeros_edge, (-1, 0)),
        ):

            @pl.when(jnp.logical_not(has[side]))
            def _():
                for k in range(2):
                    refs[s, k] = shape

        for ref, side in ((d1_recv, (1, -1)), (d2_recv, (-1, 1))):

            @pl.when(jnp.logical_not(has[side]))
            def _():
                ref[s] = zeros_edge

    def frame(ref, i, j):
        xs = {-1: (0, EDGE), 0: (EDGE, rows_x), 1: (EDGE + rows_x, EDGE)}[i]
        ys = {-1: range(WIDTH), 0: range(WIDTH, WIDTH + rows_y), 1: range(WIDTH + rows_y, 2 * WIDTH + rows_y)}[j]
        return xs, ys

    ones_slab = jnp.ones((rows_x, 128), jnp.float32)
    over_rows(lambda y: covered.__setitem__((own(y + WIDTH), slice(None)), ones_slab))
    for i, j in SIDES:
        xs, ys = frame(covered, i, j)
        inside = jnp.where(has[i, j], jnp.float32(1.0), jnp.float32(0.0))
        filler = jnp.zeros((xs[1], 128), jnp.float32) + inside
        for y in ys:
            covered[rows(y, *xs), :] = filler

    for k in range(2):
        for refs, side in ((xf_recv.at[k], (2 * k - 1, 0)), (yf_recv.at[k], (0, 2 * k - 1))):

            @pl.when(jnp.logical_not(has[side]))
            def _():
                refs[...] = jnp.zeros(refs.shape, jnp.float32)

        for j in range(2):

            @pl.when(jnp.logical_not(has[2 * k - 1, 2 * j - 1]))
            def _():
                cf_recv[k, j] = jnp.zeros((WIDTH, EDGE, 128), jnp.float32)

    loads[7].wait()
    radii = v_radius[...].astype(jnp.float32)
    for y in range(rows_y):
        weight_radius[y] = jnp.broadcast_to(radii[:, y : y + 1], (rows_x, 128))

    distances = sorted({a * a + b * b for a in range(RMAX) for b in range(RMAX) if a * a + b * b < RMAX * RMAX})

    def filtered_sum(ref, emit):
        def pair(y):
            for a in range(1, RMAX):
                sums[a - 1, y] = (
                    ref[rows(y, EDGE + a), :] + ref[rows(y, EDGE - a), :]
                )

        over_rows(pair, rows_y + 2 * WIDTH)

        def gather(y):
            def column(a, b):
                if a == 0:
                    return ref[own(y + WIDTH + b), :]
                return sums[a - 1, y + WIDTH + b]

            by_distance = {}
            for a in range(RMAX):
                for b in range(RMAX):
                    d = a * a + b * b
                    if d not in distances:
                        continue
                    term = column(a, 0) if b == 0 else column(a, b) + column(a, -b)
                    by_distance[d] = by_distance[d] + term if d in by_distance else term
            radius = weight_radius[y]
            total = radius * by_distance[0]
            for d in distances[1:]:
                total = total + jnp.maximum(radius - math.sqrt(d), 0.0) * by_distance[d]
            emit(y, total)

        over_rows(gather)

    filtered_sum(covered, lambda y, total: inv_denom.__setitem__(y, 1.0 / total))

    for load in loads[:7]:
        load.wait()

    def native(ref, y):
        return ref[pl.ds(y, rows_x, stride=rows_y), :]

    def stage(y):
        for c in range(3):
            efield[0, c, own(y), :] = native(v_electric.at[ORDER[c]], y)
        inv_eps[y] = 1.0 / (1.0 + (EPS_MATERIAL - 1.0) * native(v_density, y))

    over_rows(stage)

    def column_of(ref, x, first):
        return ref.at[pl.ds(first * slab + EDGE + x, rows_y, stride=slab), :]

    behind_mask_x = jnp.where(has[-1, 0], jnp.float32(COURANT), jnp.float32(0.0))
    behind_mask_y = jnp.where(has[0, -1], jnp.float32(COURANT), jnp.float32(0.0))

    def copies(s):
        base = 6 * s

        def copy(k, src, dst, side):
            return pltpu.make_async_remote_copy(
                src_ref=src,
                dst_ref=dst,
                send_sem=send_sems.at[base + k],
                recv_sem=recv_sems.at[base + k],
                device_id=device(*side),
                device_id_type=MESH,
            )

        return [
            ((-1, 0), copy(0, xe_send.at[s], xe_recv.at[s], (-1, 0))),
            ((1, 0), copy(1, xh_send.at[s], xh_recv.at[s], (1, 0))),
            ((0, -1), copy(2, efield.at[s, 0:2, own(0), :], ye_recv.at[s], (0, -1))),
            ((0, 1), copy(3, yh_send.at[s], yh_recv.at[s], (0, 1))),
            ((-1, 1), copy(4, xe_send.at[s, 1], d1_recv.at[s], (-1, 1))),
            (
                (1, -1),
                copy(
                    5,
                    efield.at[s, 0, edge(0, rows_x), :],
                    d2_recv.at[s],
                    (1, -1),
                ),
            ),
        ]

    def start(pairs):
        for side, copy in pairs:
            pl.when(has[side])(copy.start)

    def arrive(pairs):
        for (i, j), copy in pairs:
            pl.when(has[-i, -j])(copy.wait_recv)

    def sent(pairs):
        for side, copy in pairs:
            pl.when(has[side])(copy.wait_send)

    pending = []
    for s in range(STEPS):

        def curl_e(y, s=s):
            ex, ez, ey = (efield[s, c, own(y), :] for c in range(3))
            ex_y, ez_y = (efield[s, c, own(y + 1), :] for c in (0, 1))
            ez_x, ey_x = (efield[s, c, rows(y, EDGE + 1), :] for c in (1, 2))
            if s == 0:
                hx, hz, hy = (native(v_magnetic.at[ORDER[c]], y) for c in range(3))
            else:
                hx, hz, hy = (hfield[s - 1, c, own(y + 1), :] for c in range(3))
            hfield[s, 0, own(y + 1), :] = hx - COURANT * ((ez_y - ez) - (ahead_z(ey) - ey))
            hfield[s, 2, own(y + 1), :] = hy - COURANT * ((ahead_z(ex) - ex) - (ez_x - ez))
            hfield[s, 1, own(y + 1), :] = hz - COURANT * ((ey_x - ey) - (ex_y - ex))

        over_rows(curl_e)
        for k in range(2):
            xe_send[s, k] = column_of(efield.at[s, 1 + k], 0, 0)[...]
            xh_send[s, k] = column_of(hfield.at[s, 1 + k], rows_x - 1, 1)[...]
            yh_send[s, k] = hfield[s, k, own(rows_y), :]

        if s == 0:
            pl.semaphore_wait(barrier, greeted)
        pairs = copies(s)
        start(pairs)
        arrive(pairs)
        pending += pairs

        hfield[s, 0, own(rows_y), :] = hfield[s, 0, own(rows_y), :] - COURANT * ye_recv[s, 1]
        hfield[s, 1, own(rows_y), :] = hfield[s, 1, own(rows_y), :] + COURANT * ye_recv[s, 0]
        last_z = column_of(hfield.at[s, 1], rows_x - 1, 1)
        last_y = column_of(hfield.at[s, 2], rows_x - 1, 1)
        last_z[...] = last_z[...] - COURANT * xe_recv[s, 1]
        last_y[...] = last_y[...] + COURANT * xe_recv[s, 0]
        hfield[s, 0, own(0), :] = yh_recv[s, 0] - behind_mask_y * efield[s, 1, own(0), :]
        hfield[s, 1, own(0), :] = yh_recv[s, 1] + behind_mask_y * efield[s, 0, own(0), :]
        corner = hfield[s, 1, rows(0, EDGE + rows_x - 1, 1), :]
        hfield[s, 1, rows(0, EDGE + rows_x - 1, 1), :] = corner - COURANT * d1_recv[s, rows_y - 1 : rows_y, :]
        row = lax.broadcasted_iota(jnp.int32, (rows_y, 128), 0)
        extra = jnp.where(row == rows_y - 1, d2_recv[s, EDGE - 1 : EDGE, :], 0.0)
        column_of(hfield.at[s, 1], -1, 1)[...] = xh_recv[s, 0] - behind_mask_x * xe_send[s, 1] + COURANT * extra
        column_of(hfield.at[s, 2], -1, 1)[...] = xh_recv[s, 1] + behind_mask_x * xe_send[s, 0]

        def curl_h(y, s=s):
            hx, hz, hy = (hfield[s, c, own(y + 1), :] for c in range(3))
            hx_y, hz_y = (hfield[s, c, own(y), :] for c in (0, 1))
            hz_x, hy_x = (hfield[s, c, rows(y + 1, EDGE - 1), :] for c in (1, 2))
            curls = (
                (hz - hz_y) - (hy - behind_z(hy)),
                (hy - hy_x) - (hx - hx_y),
                (hx - behind_z(hx)) - (hz - hz_x),
            )
            material = native(v_density, y)
            scale = inv_eps[y]
            total = None
            for c in range(3):
                e = efield[s, c, own(y), :]
                if s == 0:
                    p, q = native(v_polar.at[ORDER[c]], y), native(v_rate.at[ORDER[c]], y)
                else:
                    p, q = polar[c, y], rate[c, y]
                q = DAMPING * q - OMEGA_SQUARED * p + (OMEGA_SQUARED * LORENTZ_STRENGTH) * material * e
                e = e + (COURANT * curls[c] - q) * scale
                if s + 1 < STEPS:
                    polar[c, y] = p + q
                    rate[c, y] = q
                    efield[s + 1, c, own(y), :] = e
                else:
                    o_electric[ORDER[c], pl.ds(y, rows_x, stride=rows_y), :] = e
                    o_magnetic[ORDER[c], pl.ds(y, rows_x, stride=rows_y), :] = (hx, hz, hy)[c]
                term = e * native(v_forward.at[3 * s + ORDER[c]], y)
                total = term if total is None else total + term
            if s == 0:
                gradient[y] = total
            else:
                total = gradient[y] + total
                gradient[y] = total
            if s + 1 == STEPS:
                g_send[pl.ds(y, rows_x, stride=rows_y), :] = total

        over_rows(curl_h)

    flip = pltpu.make_async_remote_copy(
        src_ref=g_send,
        dst_ref=g_recv,
        send_sem=send_sems.at[12],
        recv_sem=recv_sems.at[12],
        device_id=mirror,
        device_id_type=MESH,
    )
    flip.start()
    stores = [
        pltpu.make_async_copy(o_electric, electric_out, out_sems.at[0]),
        pltpu.make_async_copy(o_magnetic, magnetic_out, out_sems.at[1]),
        pltpu.make_async_copy(o_density, density_out, out_sems.at[2]),
    ]
    stores[0].start()
    stores[1].start()
    flip.wait_recv()

    def turn(x):
        g_flip[pl.ds(pl.multiple_of(x * rows_y, rows_y), rows_y), :] = g_recv[
            pl.ds(pl.multiple_of((rows_x - 1 - x) * rows_y, rows_y), rows_y), :
        ]

    over_rows(turn, rows_x)

    def update(y):
        mirrored = g_flip[pl.ds(partner_in[y], rows_x, stride=rows_y), :]
        symmetric = 0.5 * (gradient[y] + mirrored)
        design = native(v_mask, y).astype(jnp.float32)
        updated[own(y + WIDTH), :] = native(v_density, y) - UPDATE_STEP * design * symmetric

    over_rows(update)

    for r in range(WIDTH):
        xf_send[0, r] = column_of(updated, r, WIDTH)[...]
        xf_send[1, r] = column_of(updated, rows_x - WIDTH + r, WIDTH)[...]
        yf_send[0, r] = updated[own(WIDTH + r), :]
        yf_send[1, r] = updated[own(rows_y + r), :]

    halos = []
    for k, (i, j) in enumerate(SIDES):
        if j == 0:
            src, dst = xf_send.at[(i + 1) // 2], xf_recv.at[(1 - i) // 2]
        elif i == 0:
            src, dst = yf_send.at[(j + 1) // 2], yf_recv.at[(1 - j) // 2]
        else:
            xs = slice(0, EDGE) if i < 0 else slice(rows_x - EDGE, rows_x)
            src, dst = yf_send.at[(j + 1) // 2, :, xs, :], cf_recv.at[(1 - i) // 2, (1 - j) // 2]
        halos.append(
            (
                (i, j),
                pltpu.make_async_remote_copy(
                    src_ref=src,
                    dst_ref=dst,
                    send_sem=send_sems.at[13 + k],
                    recv_sem=recv_sems.at[13 + k],
                    device_id=device(i, j),
                    device_id_type=MESH,
                ),
            )
        )
    start(halos)
    arrive(halos)
    for r in range(WIDTH):
        column_of(updated, r - WIDTH, WIDTH)[...] = xf_recv[0, r]
        column_of(updated, rows_x + r, WIDTH)[...] = xf_recv[1, r]
        for j in range(2):
            y = r + j * (WIDTH + rows_y)
            updated[own(y), :] = yf_recv[j, r]
            updated[edge(y, 0), :] = cf_recv[0, j, r]
            updated[edge(y, EDGE + rows_x), :] = cf_recv[1, j, r]

    top = math.tanh(SHARPNESS * THRESHOLD)
    bottom = top + math.tanh(SHARPNESS * (1.0 - THRESHOLD))

    def project(y, total):
        filtered = total * inv_denom[y]
        o_density[pl.ds(y, rows_x, stride=rows_y), :] = (
            top + jnp.tanh(SHARPNESS * (filtered - THRESHOLD))
        ) / bottom

    filtered_sum(updated, project)
    stores[2].start()
    sent(pending)
    flip.wait_send()
    sent(halos)
    for store in stores:
        store.wait()


def local(nx, ny, *args):
    rows_x, rows_y, depth = args[4].shape
    cells = rows_x * rows_y
    slab = rows_x + 2 * EDGE
    f32 = jnp.float32

    def vmem(*shape, dtype=f32):
        return pltpu.VMEM(shape, dtype)

    any_spec = pl.BlockSpec(memory_space=pl.ANY)
    electric, magnetic, polar, rate, density, forward, mask, partner, radius = args
    operands = (
        electric.reshape(3, cells, depth),
        magnetic.reshape(3, cells, depth),
        polar.reshape(3, cells, depth),
        rate.reshape(3, cells, depth),
        density.reshape(cells, depth),
        forward.reshape(3 * STEPS, cells, depth),
        mask.reshape(cells, depth),
        partner,
        radius,
    )
    in_specs = [any_spec] * 7 + [pl.BlockSpec(memory_space=pltpu.SMEM), any_spec]
    outs = pl.pallas_call(
        functools.partial(kernel, nx, ny),
        out_shape=(
            jax.ShapeDtypeStruct((3, cells, depth), f32),
            jax.ShapeDtypeStruct((3, cells, depth), f32),
            jax.ShapeDtypeStruct((cells, depth), f32),
        ),
        in_specs=in_specs,
        out_specs=(any_spec, any_spec, any_spec),
        scratch_shapes=[
            vmem(3, cells, depth),
            vmem(3, cells, depth),
            vmem(3, cells, depth),
            vmem(3, cells, depth),
            vmem(cells, depth),
            vmem(3 * STEPS, cells, depth),
            vmem(cells, depth, dtype=jnp.int32),
            vmem(rows_x, rows_y, dtype=jnp.int32),
            vmem(STEPS, 3, (rows_y + 1) * slab, depth),
            vmem(STEPS, 3, (rows_y + 1) * slab, depth),
            vmem(3, rows_y, rows_x, depth),
            vmem(3, rows_y, rows_x, depth),
            vmem(rows_y, rows_x, depth),
            vmem(rows_y, rows_x, depth),
            vmem(cells, depth),
            vmem(cells, depth),
            vmem(cells, depth),
            vmem((rows_y + 2 * WIDTH) * slab, depth),
            vmem((rows_y + 2 * WIDTH) * slab, depth),
            vmem(WIDTH, rows_y + 2 * WIDTH, rows_x, depth),
            vmem(rows_y, rows_x, depth),
            vmem(rows_y, rows_x, depth),
            vmem(STEPS, 2, rows_x, depth),
            vmem(STEPS, 2, rows_x, depth),
            vmem(STEPS, 2, rows_x, depth),
            vmem(STEPS, 2, rows_y, depth),
            vmem(STEPS, 2, rows_y, depth),
            vmem(STEPS, 2, rows_y, depth),
            vmem(STEPS, 2, rows_y, depth),
            vmem(STEPS, EDGE, depth),
            vmem(STEPS, EDGE, depth),
            vmem(2, WIDTH, rows_y, depth),
            vmem(2, WIDTH, rows_y, depth),
            vmem(2, WIDTH, rows_x, depth),
            vmem(2, WIDTH, rows_x, depth),
            vmem(2, 2, WIDTH, EDGE, depth),
            vmem(3, cells, depth),
            vmem(3, cells, depth),
            vmem(cells, depth),
            pltpu.SemaphoreType.DMA((8,)),
            pltpu.SemaphoreType.DMA((3,)),
            pltpu.SemaphoreType.DMA((21,)),
            pltpu.SemaphoreType.DMA((21,)),
        ],
        compiler_params=pltpu.CompilerParams(collective_id=0, has_side_effects=True),
    )(*operands)
    return (
        outs[0].reshape(electric.shape),
        outs[1].reshape(magnetic.shape),
        outs[2].reshape(density.shape),
    )


def solution(mesh):
    in_specs = (
        P(None, "gx", "gy", None),
        P(None, "gx", "gy", None),
        P(None, "gx", "gy", None),
        P(None, "gx", "gy", None),
        P("gx", "gy", None),
        P(None, None, "gx", "gy", None),
        P("gx", "gy", None),
        P("gy"),
        P("gx", "gy"),
    )
    out_specs = (P(None, "gx", "gy", None), P(None, "gx", "gy", None), P("gx", "gy", None))
    return jax.shard_map(
        functools.partial(local, mesh.shape["gx"], mesh.shape["gy"]),
        mesh=mesh,
        in_specs=in_specs,
        out_specs=out_specs,
        check_vma=False,
    )
```

time: 134 us -> 61.1 us (0.46)
  the two profiles are of different devices: /device:TPU:39 before, /device:TPU:57 now
where the time goes in v1:
time: 61.1 us; the launch traced here: 60.9 us
  Pallas kernels  55.4 us (91%)
  local copies, waits for them, and re-layouts  4.86 us (8%)
  between operations  0.66 us (1%)
    pallas_call x1, Pallas kernels, local(): pl.pallas_call(functools.partial(kernel, nx, ny), out_shape=(jax.ShapeDty...  55.4 us
    unnamed x10, local copies, waits for them, and re-layouts  4.86 us

profile of v1, /device:TPU:57, one launch (start us, length us, event | category | flops | bytes accessed | tf_op | source)
XLA Modules:
  0.0 60.9 jit_solution(16328387022469954843)
XLA Ops:
  0.6 0.0 copy-start.2
  0.6 0.7 %copy-done.2 = s32[32,8]{0,1:T(8,128)S(1)} copy-done((s32[32,8]{0,1:T(8,128)S(1)}, s32[32,8]{0,1:T(8,128)}, u32[]{:S(2)}) %copy-start.2) | copy-done | bytes 1048
  1.3 0.7 %copy.12.radius_in = s32[32,8]{1,0:T(8,128)} copy(s32[32,8]{0,1:T(8,128)S(1)} %copy-done.2) | data formatting | bytes 2048 | tf_op args[8]
  2.0 55.4 %shard_map.112 = (f32[3,256,128]{2,1,0:T(8,128)}, f32[3,256,128]{2,1,0:T(8,128)}, f32[256,128]{1,0:T(8,128)}) custom-call(f32[3,256,128]{2,1,0:T(8,128)} %bitcast.13, f32[3,256,128]{2,1,0:T(8,128)} %bitcast.14, f32[3,256,128]{2,1,0:T(8,128)} %bitcast.15, f32[3,256,128]{2,1,0:T(8,128)} %bitcast.16, f32[256,128]{1,0:T(8,128)} %bitcast.17, ...), custom_call_target="tpu_custom_call" | custom-call | tf_op jit(solution)/shard_map/pallas_call | solution.py:514
  57.4 0.0 copy-start
  57.4 1.8 %copy.16 = f32[3,32,8,128]{3,2,1,0:T(8,128)} copy(f32[3,32,8,128]{3,2,1,0:T(8,128)} %bitcast.12) | data formatting | bytes 786432
  59.2 0.0 copy-done
  59.2 0.0 copy-start.1
  59.2 0.7 %copy.17 = f32[3,32,8,128]{3,2,1,0:T(8,128)} copy(f32[3,32,8,128]{3,2,1,0:T(8,128)S(1)} %bitcast.11) | data formatting | bytes 786432
  60.0 0.3 copy-done.1
  60.2 0.7 %copy.18 = f32[32,8,128]{2,1,0:T(8,128)} copy(f32[32,8,128]{2,1,0:T(8,128)S(1)} %bitcast.19) | data formatting | bytes 262144
Async XLA Ops:
  0.6 0.7 %copy-start.2 = (s32[32,8]{0,1:T(8,128)S(1)}, s32[32,8]{0,1:T(8,128)}, u32[]{:S(2)}) copy-start(s32[32,8]{0,1:T(8,128)} %param.17) | copy-start | bytes 3076
  57.4 1.8 %copy-start = (f32[3,256,128]{2,1,0:T(8,128)S(1)}, f32[3,256,128]{2,1,0:T(8,128)}, u32[]{:S(2)}) copy-start(f32[3,256,128]{2,1,0:T(8,128)} %get-tuple-element.7) | copy-start | bytes 1179652
  59.2 1.0 %copy-start.1 = (f32[256,128]{1,0:T(8,128)S(1)}, f32[256,128]{1,0:T(8,128)}, u32[]{:S(2)}) copy-start(f32[256,128]{1,0:T(8,128)} %get-tuple-element.8) | copy-start | bytes 393220

commit v2 on v1

--- a/solution.py
+++ b/solution.py
@@ -38,9 +38,9 @@
     mask_in,
     partner_in,
     radius_in,
-    electric_out,
-    magnetic_out,
-    density_out,
+    o_electric,
+    o_magnetic,
+    o_density,
     v_electric,
     v_magnetic,
     v_polar,
@@ -53,6 +53,7 @@
     hfield,
     polar,
     rate,
+    driven,
     inv_eps,
     gradient,
     g_send,
@@ -77,15 +78,11 @@
     yf_send,
     yf_recv,
     cf_recv,
-    o_electric,
-    o_magnetic,
-    o_density,
     in_sems,
-    out_sems,
     send_sems,
     recv_sems,
 ):
-    rows_x, rows_y = v_radius.shape
+    rows_y, rows_x = v_radius.shape
     slab = rows_x + 2 * EDGE
 
     def rows(y, first=EDGE, count=rows_x):
@@ -169,56 +166,17 @@
 
             over_rows(clear)
 
-    for s in range(STEPS):
-        for refs, shape, side in (
-            (ye_recv, zeros_slab, (0, 1)),
-            (yh_recv, zeros_slab, (0, -1)),
-            (xe_recv, zeros_edge, (1, 0)),
-            (xh_recv, zeros_edge, (-1, 0)),
-        ):
-
-            @pl.when(jnp.logical_not(has[side]))
-            def _():
-                for k in range(2):
-                    refs[s, k] = shape
-
-        for ref, side in ((d1_recv, (1, -1)), (d2_recv, (-1, 1))):
-
-            @pl.when(jnp.logical_not(has[side]))
-            def _():
-                ref[s] = zeros_edge
-
-    def frame(ref, i, j):
-        xs = {-1: (0, EDGE), 0: (EDGE, rows_x), 1: (EDGE + rows_x, EDGE)}[i]
-        ys = {-1: range(WIDTH), 0: range(WIDTH, WIDTH + rows_y), 1: range(WIDTH + rows_y, 2 * WIDTH + rows_y)}[j]
-        return xs, ys
-
-    ones_slab = jnp.ones((rows_x, 128), jnp.float32)
-    over_rows(lambda y: covered.__setitem__((own(y + WIDTH), slice(None)), ones_slab))
-    for i, j in SIDES:
-        xs, ys = frame(covered, i, j)
-        inside = jnp.where(has[i, j], jnp.float32(1.0), jnp.float32(0.0))
-        filler = jnp.zeros((xs[1], 128), jnp.float32) + inside
-        for y in ys:
-            covered[rows(y, *xs), :] = filler
-
-    for k in range(2):
-        for refs, side in ((xf_recv.at[k], (2 * k - 1, 0)), (yf_recv.at[k], (0, 2 * k - 1))):
-
-            @pl.when(jnp.logical_not(has[side]))
-            def _():
-                refs[...] = jnp.zeros(refs.shape, jnp.float32)
-
-        for j in range(2):
-
-            @pl.when(jnp.logical_not(has[2 * k - 1, 2 * j - 1]))
-            def _():
-                cf_recv[k, j] = jnp.zeros((WIDTH, EDGE, 128), jnp.float32)
-
-    loads[7].wait()
-    radii = v_radius[...].astype(jnp.float32)
-    for y in range(rows_y):
-        weight_radius[y] = jnp.broadcast_to(radii[:, y : y + 1], (rows_x, 128))
+    def native(ref, y):
+        return ref[pl.ds(y, rows_x, stride=rows_y), :]
+
+    loads[0].wait()
+
+    def stage(y):
+        for c in range(3):
+            efield[0, c, own(y), :] = native(v_electric.at[ORDER[c]], y)
+
+    over_rows(stage)
+    loads[1].wait()
 
     distances = sorted({a * a + b * b for a in range(RMAX) for b in range(RMAX) if a * a + b * b < RMAX * RMAX})
 
@@ -253,20 +211,61 @@
 
         over_rows(gather)
 
-    filtered_sum(covered, lambda y, total: inv_denom.__setitem__(y, 1.0 / total))
-
-    for load in loads[:7]:
-        load.wait()
-
-    def native(ref, y):
-        return ref[pl.ds(y, rows_x, stride=rows_y), :]
-
-    def stage(y):
-        for c in range(3):
-            efield[0, c, own(y), :] = native(v_electric.at[ORDER[c]], y)
-        inv_eps[y] = 1.0 / (1.0 + (EPS_MATERIAL - 1.0) * native(v_density, y))
-
-    over_rows(stage)
+    def settle():
+        for s in range(STEPS):
+            for refs, shape, side in (
+                (ye_recv, zeros_slab, (0, 1)),
+                (yh_recv, zeros_slab, (0, -1)),
+                (xe_recv, zeros_edge, (1, 0)),
+                (xh_recv, zeros_edge, (-1, 0)),
+            ):
+
+                @pl.when(jnp.logical_not(has[side]))
+                def _():
+                    for k in range(2):
+                        refs[s, k] = shape
+
+            for ref, side in ((d1_recv, (1, -1)), (d2_recv, (-1, 1))):
+
+                @pl.when(jnp.logical_not(has[side]))
+                def _():
+                    ref[s] = zeros_edge
+
+        def frame(ref, i, j):
+            xs = {-1: (0, EDGE), 0: (EDGE, rows_x), 1: (EDGE + rows_x, EDGE)}[i]
+            ys = {-1: range(WIDTH), 0: range(WIDTH, WIDTH + rows_y), 1: range(WIDTH + rows_y, 2 * WIDTH + rows_y)}[j]
+            return xs, ys
+
+        ones_slab = jnp.ones((rows_x, 128), jnp.float32)
+        over_rows(lambda y: covered.__setitem__((own(y + WIDTH), slice(None)), ones_slab))
+        for i, j in SIDES:
+            xs, ys = frame(covered, i, j)
+            inside = jnp.where(has[i, j], jnp.float32(1.0), jnp.float32(0.0))
+            filler = jnp.zeros((xs[1], 128), jnp.float32) + inside
+            for y in ys:
+                covered[rows(y, *xs), :] = filler
+
+        for k in range(2):
+            for refs, side in ((xf_recv.at[k], (2 * k - 1, 0)), (yf_recv.at[k], (0, 2 * k - 1))):
+
+                @pl.when(jnp.logical_not(has[side]))
+                def _():
+                    refs[...] = jnp.zeros(refs.shape, jnp.float32)
+
+            for j in range(2):
+
+                @pl.when(jnp.logical_not(has[2 * k - 1, 2 * j - 1]))
+                def _():
+                    cf_recv[k, j] = jnp.zeros((WIDTH, EDGE, 128), jnp.float32)
+
+        loads[7].wait()
+        radii = v_radius[...].astype(jnp.float32).T
+        for y in range(rows_y):
+            weight_radius[y] = jnp.broadcast_to(radii[:, y : y + 1], (rows_x, 128))
+
+        filtered_sum(covered, lambda y, total: inv_denom.__setitem__(y, 1.0 / total))
+        for load in loads[2:7]:
+            load.wait()
 
     def column_of(ref, x, first):
         return ref.at[pl.ds(first * slab + EDGE + x, rows_y, stride=slab), :]
@@ -341,6 +340,27 @@
             pl.semaphore_wait(barrier, greeted)
         pairs = copies(s)
         start(pairs)
+        if s == 0:
+            settle()
+
+        def drive(y, s=s):
+            if s == 0:
+                inv_eps[y] = 1.0 / (1.0 + (EPS_MATERIAL - 1.0) * native(v_density, y))
+            material = (OMEGA_SQUARED * LORENTZ_STRENGTH) * native(v_density, y)
+            scale = inv_eps[y]
+            for c in range(3):
+                e = efield[s, c, own(y), :]
+                if s == 0:
+                    p, q = native(v_polar.at[ORDER[c]], y), native(v_rate.at[ORDER[c]], y)
+                else:
+                    p, q = polar[c, y], rate[c, y]
+                q = DAMPING * q - OMEGA_SQUARED * p + material * e
+                if s + 1 < STEPS:
+                    polar[c, y] = p + q
+                    rate[c, y] = q
+                driven[c, y] = e - q * scale
+
+        over_rows(drive)
         arrive(pairs)
         pending += pairs
 
@@ -368,20 +388,11 @@
                 (hy - hy_x) - (hx - hx_y),
                 (hx - behind_z(hx)) - (hz - hz_x),
             )
-            material = native(v_density, y)
-            scale = inv_eps[y]
+            scale = COURANT * inv_eps[y]
             total = None
             for c in range(3):
-                e = efield[s, c, own(y), :]
-                if s == 0:
-                    p, q = native(v_polar.at[ORDER[c]], y), native(v_rate.at[ORDER[c]], y)
-                else:
-                    p, q = polar[c, y], rate[c, y]
-                q = DAMPING * q - OMEGA_SQUARED * p + (OMEGA_SQUARED * LORENTZ_STRENGTH) * material * e
-                e = e + (COURANT * curls[c] - q) * scale
+                e = driven[c, y] + curls[c] * scale
                 if s + 1 < STEPS:
-                    polar[c, y] = p + q
-                    rate[c, y] = q
                     efield[s + 1, c, own(y), :] = e
                 else:
                     o_electric[ORDER[c], pl.ds(y, rows_x, stride=rows_y), :] = e
@@ -407,13 +418,6 @@
         device_id_type=MESH,
     )
     flip.start()
-    stores = [
-        pltpu.make_async_copy(o_electric, electric_out, out_sems.at[0]),
-        pltpu.make_async_copy(o_magnetic, magnetic_out, out_sems.at[1]),
-        pltpu.make_async_copy(o_density, density_out, out_sems.at[2]),
-    ]
-    stores[0].start()
-    stores[1].start()
     flip.wait_recv()
 
     def turn(x):
@@ -480,10 +484,16 @@
         ) / bottom
 
     filtered_sum(updated, project)
-    stores[2].start()
     sent(pending)
     flip.wait_send()
     sent(halos)
+
+
+def write_out(electric, magnetic, density, electric_out, magnetic_out, density_out, sems):
+    pairs = ((electric, electric_out), (magnetic, magnetic_out), (density, density_out))
+    stores = [pltpu.make_async_copy(src, dst, sems.at[k]) for k, (src, dst) in enumerate(pairs)]
+    for store in stores:
+        store.start()
     for store in stores:
         store.wait()
 
@@ -508,18 +518,16 @@
         forward.reshape(3 * STEPS, cells, depth),
         mask.reshape(cells, depth),
         partner,
-        radius,
+        radius.T,
     )
     in_specs = [any_spec] * 7 + [pl.BlockSpec(memory_space=pltpu.SMEM), any_spec]
-    outs = pl.pallas_call(
+    shapes = ((3, cells, depth), (3, cells, depth), (cells, depth))
+    vmem_spec = pl.BlockSpec(memory_space=pltpu.VMEM)
+    held = pl.pallas_call(
         functools.partial(kernel, nx, ny),
-        out_shape=(
-            jax.ShapeDtypeStruct((3, cells, depth), f32),
-            jax.ShapeDtypeStruct((3, cells, depth), f32),
-            jax.ShapeDtypeStruct((cells, depth), f32),
-        ),
+        out_shape=tuple(pltpu.VMEM(shape, f32) for shape in shapes),
         in_specs=in_specs,
-        out_specs=(any_spec, any_spec, any_spec),
+        out_specs=(vmem_spec,) * 3,
         scratch_shapes=[
             vmem(3, cells, depth),
             vmem(3, cells, depth),
@@ -528,9 +536,10 @@
             vmem(cells, depth),
             vmem(3 * STEPS, cells, depth),
             vmem(cells, depth, dtype=jnp.int32),
-            vmem(rows_x, rows_y, dtype=jnp.int32),
+            vmem(rows_y, rows_x, dtype=jnp.int32),
             vmem(STEPS, 3, (rows_y + 1) * slab, depth),
             vmem(STEPS, 3, (rows_y + 1) * slab, depth),
+            vmem(3, rows_y, rows_x, depth),
             vmem(3, rows_y, rows_x, depth),
             vmem(3, rows_y, rows_x, depth),
             vmem(rows_y, rows_x, depth),
@@ -557,16 +566,19 @@
             vmem(2, WIDTH, rows_x, depth),
             vmem(2, WIDTH, rows_x, depth),
             vmem(2, 2, WIDTH, EDGE, depth),
-            vmem(3, cells, depth),
-            vmem(3, cells, depth),
-            vmem(cells, depth),
             pltpu.SemaphoreType.DMA((8,)),
-            pltpu.SemaphoreType.DMA((3,)),
             pltpu.SemaphoreType.DMA((21,)),
             pltpu.SemaphoreType.DMA((21,)),
         ],
         compiler_params=pltpu.CompilerParams(collective_id=0, has_side_effects=True),
     )(*operands)
+    outs = pl.pallas_call(
+        write_out,
+        out_shape=tuple(jax.ShapeDtypeStruct(shape, f32) for shape in shapes),
+        in_specs=[vmem_spec] * 3,
+        out_specs=(any_spec,) * 3,
+        scratch_shapes=[pltpu.SemaphoreType.DMA((3,))],
+    )(*[pltpu.with_memory_space_constraint(a, pltpu.VMEM) for a in held])
     return (
         outs[0].reshape(electric.shape),
         outs[1].reshape(magnetic.shape),

time: 61.1 us -> 55 us (0.900); the launches traced: 60.9 us -> 54 us
  local copies, waits for them, and re-layouts: 4.86 us -> 0 us
  Pallas kernels: 55.4 us -> 53.4 us
    unnamed x10 -> x0, local copies, waits for them, and re-layouts: 4.86 us -> none
    pallas_call x1 -> x2, Pallas kernels: 55.4 us -> 53.4 us  [the longest x1 52.4 us: local(): pl.pallas_call(functools.partial(kernel, nx, ny), out_shape=tuple((pltpu....]
where the time goes in v2:
time: 55 us; the launch traced here: 54 us
  Pallas kernels  53.4 us (97%)
  between operations  0.64 us (1%)
    pallas_call x1, Pallas kernels, local(): pl.pallas_call(functools.partial(kernel, nx, ny), out_shape=tuple((pltpu....  52.4 us

profile of v2, /device:TPU:57, one launch (start us, length us, event | category | flops | bytes accessed | tf_op | source)
XLA Modules:
  0.0 54.0 jit_solution(11500840185871229994)
XLA Ops:
  0.6 52.4 %shard_map.112 = (f32[3,256,128]{2,1,0:T(8,128)S(1)}, f32[3,256,128]{2,1,0:T(8,128)S(1)}, f32[256,128]{1,0:T(8,128)S(1)}) custom-call(f32[3,256,128]{2,1,0:T(8,128)} %bitcast.12, f32[3,256,128]{2,1,0:T(8,128)} %bitcast.13, f32[3,256,128]{2,1,0:T(8,128)} %bitcast.14, f32[3,256,128]{2,1,0:T(8,128)} %bitcast.15, f32[256,128]{1,0:T(8,128)} %bitcast.16, ...), custom_call_target="tpu_custom_call" | custom-call | tf_op jit(solution)/shard_map/pallas_call | solution.py:526
  53.1 0.9 %shard_map.113 = (f32[3,256,128]{2,1,0:T(8,128)}, f32[3,256,128]{2,1,0:T(8,128)}, f32[256,128]{1,0:T(8,128)}) custom-call(f32[3,256,128]{2,1,0:T(8,128)S(1)} %get-tuple-element.9.electric, f32[3,256,128]{2,1,0:T(8,128)S(1)} %get-tuple-element.10.magnetic, f32[256,128]{1,0:T(8,128)S(1)} %get-tuple-element.11.density), custom_call_target="tpu_custom_call" | custom-call | tf_op jit(solution)/shard_map/pallas_call | solution.py:575

commit v3 on v2

--- a/solution.py
+++ b/solution.py
@@ -54,11 +54,15 @@
     polar,
     rate,
     driven,
+    kept,
     inv_eps,
     gradient,
     g_send,
     g_recv,
+    g_turn,
     g_flip,
+    ends_send,
+    ends_recv,
     updated,
     covered,
     sums,
@@ -148,12 +152,12 @@
     def behind_z(v):
         return jnp.where(lane > 0, pltpu.roll(v, 1, 1), 0.0)
 
-    def over_rows(body, count=rows_y):
+    def over_rows(body, stop=rows_y, start=0):
         def step(y, carry):
             body(y)
             return carry
 
-        lax.fori_loop(0, count, step, 0)
+        lax.fori_loop(start, stop, step, 0)
 
     zeros_slab = jnp.zeros((rows_x, 128), jnp.float32)
     zeros_edge = jnp.zeros((EDGE, 128), jnp.float32)
@@ -315,20 +319,98 @@
         for side, copy in pairs:
             pl.when(has[side])(copy.wait_send)
 
+    def column(y):
+        return pl.ds(y * rows_x if isinstance(y, int) else pl.multiple_of(y * rows_x, rows_x), rows_x)
+
+    def curled(s, y):
+        ex, ez, ey = (efield[s, c, own(y), :] for c in range(3))
+        ex_y, ez_y = (efield[s, c, own(y + 1), :] for c in (0, 1))
+        ez_x, ey_x = (efield[s, c, rows(y, EDGE + 1), :] for c in (1, 2))
+        if s == 0:
+            hx, hz, hy = (native(v_magnetic.at[ORDER[c]], y) for c in range(3))
+        else:
+            hx, hz, hy = (hfield[s - 1, c, own(y + 1), :] for c in range(3))
+        hfield[s, 0, own(y + 1), :] = hx - COURANT * ((ez_y - ez) - (ahead_z(ey) - ey))
+        hfield[s, 2, own(y + 1), :] = hy - COURANT * ((ahead_z(ex) - ex) - (ez_x - ez))
+        hfield[s, 1, own(y + 1), :] = hz - COURANT * ((ey_x - ey) - (ex_y - ex))
+
+    def driven_by(s, y, fields):
+        material = (OMEGA_SQUARED * LORENTZ_STRENGTH) * native(v_density, y)
+        scale = inv_eps[y]
+        for c in range(3):
+            if s == 0:
+                p, q = native(v_polar.at[ORDER[c]], y), native(v_rate.at[ORDER[c]], y)
+            else:
+                p, q = polar[c, y], rate[c, y]
+            q = DAMPING * q - OMEGA_SQUARED * p + material * fields[c]
+            if s + 1 < STEPS:
+                polar[c, y] = p + q
+                rate[c, y] = q
+            driven[c, y] = fields[c] - q * scale
+
+    def advanced(s, y):
+        hx, hz, hy = (hfield[s, c, own(y + 1), :] for c in range(3))
+        hx_y, hz_y = (hfield[s, c, own(y), :] for c in (0, 1))
+        hz_x, hy_x = (hfield[s, c, rows(y + 1, EDGE - 1), :] for c in (1, 2))
+        curls = (
+            (hz - hz_y) - (hy - behind_z(hy)),
+            (hy - hy_x) - (hx - hx_y),
+            (hx - behind_z(hx)) - (hz - hz_x),
+        )
+        scale = COURANT * inv_eps[y]
+        news = [driven[c, y] + curls[c] * scale for c in range(3)]
+        total = None
+        for c in range(3):
+            term = news[c] * native(v_forward.at[3 * s + ORDER[c]], y)
+            total = term if total is None else total + term
+        return (hx, hz, hy), news, total
+
+    def flip(k, src, dst):
+        return pltpu.make_async_remote_copy(
+            src_ref=src,
+            dst_ref=dst,
+            send_sem=send_sems.at[k],
+            recv_sem=recv_sems.at[k],
+            device_id=mirror,
+            device_id_type=MESH,
+        )
+
+    def inner_rows():
+        def first(y):
+            _, news, total = advanced(0, y)
+            for c in range(3):
+                efield[1, c, own(y), :] = news[c]
+            gradient[column(y), :] = total
+
+        over_rows(first, rows_y - 1, 1)
+        over_rows(lambda y: curled(1, y), rows_y - 2, 1)
+
+        def second(y):
+            material = (OMEGA_SQUARED * LORENTZ_STRENGTH) * native(v_density, y)
+            for c in range(3):
+                kept[c, y] = driven[c, y]
+                e = efield[1, c, own(y), :]
+                q = DAMPING * rate[c, y] - OMEGA_SQUARED * polar[c, y] + material * e
+                driven[c, y] = e - q * inv_eps[y]
+            _, _, total = advanced(1, y)
+            g_send[column(y), :] = gradient[column(y), :] + total
+            for c in range(3):
+                driven[c, y] = kept[c, y]
+
+        over_rows(second, rows_y - 2, 2)
+
+    inner = pl.ds(2 * rows_x, (rows_y - 4) * rows_x)
+    flips = [flip(12, g_send.at[inner, :], g_recv.at[inner, :])]
+    flips += [flip(13 + k, g_send.at[column(y), :], g_recv.at[column(y), :]) for k, y in enumerate((1, rows_y - 2))]
+    flips += [flip(15 + k, gradient.at[column(y), :], g_recv.at[column(y), :]) for k, y in enumerate((0, rows_y - 1))]
+    flips += [flip(17, ends_send, ends_recv)]
+    ends = (0, 1, rows_x - 2, rows_x - 1)
+
     pending = []
     for s in range(STEPS):
 
         def curl_e(y, s=s):
-            ex, ez, ey = (efield[s, c, own(y), :] for c in range(3))
-            ex_y, ez_y = (efield[s, c, own(y + 1), :] for c in (0, 1))
-            ez_x, ey_x = (efield[s, c, rows(y, EDGE + 1), :] for c in (1, 2))
-            if s == 0:
-                hx, hz, hy = (native(v_magnetic.at[ORDER[c]], y) for c in range(3))
-            else:
-                hx, hz, hy = (hfield[s - 1, c, own(y + 1), :] for c in range(3))
-            hfield[s, 0, own(y + 1), :] = hx - COURANT * ((ez_y - ez) - (ahead_z(ey) - ey))
-            hfield[s, 2, own(y + 1), :] = hy - COURANT * ((ahead_z(ex) - ex) - (ez_x - ez))
-            hfield[s, 1, own(y + 1), :] = hz - COURANT * ((ey_x - ey) - (ex_y - ex))
+            curled(s, y)
 
         over_rows(curl_e)
         for k in range(2):
@@ -342,25 +424,24 @@
         start(pairs)
         if s == 0:
             settle()
+            over_rows(
+                lambda y: inv_eps.__setitem__(
+                    y, 1.0 / (1.0 + (EPS_MATERIAL - 1.0) * native(v_density, y))
+                )
+            )
 
         def drive(y, s=s):
-            if s == 0:
-                inv_eps[y] = 1.0 / (1.0 + (EPS_MATERIAL - 1.0) * native(v_density, y))
-            material = (OMEGA_SQUARED * LORENTZ_STRENGTH) * native(v_density, y)
-            scale = inv_eps[y]
-            for c in range(3):
-                e = efield[s, c, own(y), :]
-                if s == 0:
-                    p, q = native(v_polar.at[ORDER[c]], y), native(v_rate.at[ORDER[c]], y)
-                else:
-                    p, q = polar[c, y], rate[c, y]
-                q = DAMPING * q - OMEGA_SQUARED * p + material * e
-                if s + 1 < STEPS:
-                    polar[c, y] = p + q
-                    rate[c, y] = q
-                driven[c, y] = e - q * scale
+            driven_by(s, y, [efield[s, c, own(y), :] for c in range(3)])
 
         over_rows(drive)
+        if s == 0:
+            inner_rows()
+            flips[0].start()
+        else:
+            for y in (1, rows_y - 2):
+                g_send[column(y), :] = gradient[column(y), :] + advanced(s, y)[2]
+            flips[1].start()
+            flips[2].start()
         arrive(pairs)
         pending += pairs
 
@@ -380,48 +461,35 @@
         column_of(hfield.at[s, 2], -1, 1)[...] = xh_recv[s, 1] + behind_mask_x * xe_send[s, 0]
 
         def curl_h(y, s=s):
-            hx, hz, hy = (hfield[s, c, own(y + 1), :] for c in range(3))
-            hx_y, hz_y = (hfield[s, c, own(y), :] for c in (0, 1))
-            hz_x, hy_x = (hfield[s, c, rows(y + 1, EDGE - 1), :] for c in (1, 2))
-            curls = (
-                (hz - hz_y) - (hy - behind_z(hy)),
-                (hy - hy_x) - (hx - hx_y),
-                (hx - behind_z(hx)) - (hz - hz_x),
-            )
-            scale = COURANT * inv_eps[y]
-            total = None
+            hs, news, total = advanced(s, y)
             for c in range(3):
-                e = driven[c, y] + curls[c] * scale
                 if s + 1 < STEPS:
-                    efield[s + 1, c, own(y), :] = e
+                    efield[s + 1, c, own(y), :] = news[c]
                 else:
-                    o_electric[ORDER[c], pl.ds(y, rows_x, stride=rows_y), :] = e
-                    o_magnetic[ORDER[c], pl.ds(y, rows_x, stride=rows_y), :] = (hx, hz, hy)[c]
-                term = e * native(v_forward.at[3 * s + ORDER[c]], y)
-                total = term if total is None else total + term
-            if s == 0:
-                gradient[y] = total
-            else:
-                total = gradient[y] + total
-                gradient[y] = total
-            if s + 1 == STEPS:
-                g_send[pl.ds(y, rows_x, stride=rows_y), :] = total
+                    o_electric[ORDER[c], pl.ds(y, rows_x, stride=rows_y), :] = news[c]
+                    o_magnetic[ORDER[c], pl.ds(y, rows_x, stride=rows_y), :] = hs[c]
+            if s > 0:
+                total = gradient[column(y), :] + total
+            gradient[column(y), :] = total
 
         over_rows(curl_h)
 
-    flip = pltpu.make_async_remote_copy(
-        src_ref=g_send,
-        dst_ref=g_recv,
-        send_sem=send_sems.at[12],
-        recv_sem=recv_sems.at[12],
-        device_id=mirror,
-        device_id_type=MESH,
-    )
-    flip.start()
-    flip.wait_recv()
+    for k, x in enumerate(ends):
+        ends_send[k] = gradient[pl.ds(x, rows_y, stride=rows_x), :]
+    for copy in flips[3:]:
+        copy.start()
+    for copy in flips:
+        copy.wait_recv()
+
+    def spread(y):
+        g_turn[pl.ds(y, rows_x, stride=rows_y), :] = g_recv[column(y), :]
+
+    over_rows(spread)
+    for k, x in enumerate(ends):
+        g_turn[pl.ds(x * rows_y, rows_y), :] = ends_recv[k]
 
     def turn(x):
-        g_flip[pl.ds(pl.multiple_of(x * rows_y, rows_y), rows_y), :] = g_recv[
+        g_flip[pl.ds(pl.multiple_of(x * rows_y, rows_y), rows_y), :] = g_turn[
             pl.ds(pl.multiple_of((rows_x - 1 - x) * rows_y, rows_y), rows_y), :
         ]
 
@@ -429,7 +497,7 @@
 
     def update(y):
         mirrored = g_flip[pl.ds(partner_in[y], rows_x, stride=rows_y), :]
-        symmetric = 0.5 * (gradient[y] + mirrored)
+        symmetric = 0.5 * (gradient[column(y), :] + mirrored)
         design = native(v_mask, y).astype(jnp.float32)
         updated[own(y + WIDTH), :] = native(v_density, y) - UPDATE_STEP * design * symmetric
 
@@ -456,8 +524,8 @@
                 pltpu.make_async_remote_copy(
                     src_ref=src,
                     dst_ref=dst,
-                    send_sem=send_sems.at[13 + k],
-                    recv_sem=recv_sems.at[13 + k],
+                    send_sem=send_sems.at[18 + k],
+                    recv_sem=recv_sems.at[18 + k],
                     device_id=device(i, j),
                     device_id_type=MESH,
                 ),
@@ -485,7 +553,8 @@
 
     filtered_sum(updated, project)
     sent(pending)
-    flip.wait_send()
+    for copy in flips:
+        copy.wait_send()
     sent(halos)
 
 
@@ -542,11 +611,15 @@
             vmem(3, rows_y, rows_x, depth),
             vmem(3, rows_y, rows_x, depth),
             vmem(3, rows_y, rows_x, depth),
-            vmem(rows_y, rows_x, depth),
+            vmem(3, rows_y, rows_x, depth),
             vmem(rows_y, rows_x, depth),
             vmem(cells, depth),
             vmem(cells, depth),
             vmem(cells, depth),
+            vmem(cells, depth),
+            vmem(cells, depth),
+            vmem(4, rows_y, depth),
+            vmem(4, rows_y, depth),
             vmem((rows_y + 2 * WIDTH) * slab, depth),
             vmem((rows_y + 2 * WIDTH) * slab, depth),
             vmem(WIDTH, rows_y + 2 * WIDTH, rows_x, depth),
@@ -567,8 +640,8 @@
             vmem(2, WIDTH, rows_x, depth),
             vmem(2, 2, WIDTH, EDGE, depth),
             pltpu.SemaphoreType.DMA((8,)),
-            pltpu.SemaphoreType.DMA((21,)),
-            pltpu.SemaphoreType.DMA((21,)),
+            pltpu.SemaphoreType.DMA((26,)),
+            pltpu.SemaphoreType.DMA((26,)),
         ],
         compiler_params=pltpu.CompilerParams(collective_id=0, has_side_effects=True),
     )(*operands)

time: 55 us -> 52 us (0.945)
  Pallas kernels: 53.4 us -> 50.8 us
    pallas_call x1, Pallas kernels: 52.4 us -> 49.8 us  [local(): pl.pallas_call(functools.partial(kernel, nx, ny), out_shape=tuple((pltpu....]
where the time goes in v3:
time: 52 us; the launch traced here: 51.4 us
  Pallas kernels  50.8 us (98%)
  between operations  0.64 us (1%)
    pallas_call x1, Pallas kernels, local(): pl.pallas_call(functools.partial(kernel, nx, ny), out_shape=tuple((pltpu....  49.8 us

profile of v3, /device:TPU:57, one launch (start us, length us, event | category | flops | bytes accessed | tf_op | source)
XLA Modules:
  0.0 51.4 jit_solution(11031090525331033595)
XLA Ops:
  0.6 49.8 %shard_map.112 = (f32[3,256,128]{2,1,0:T(8,128)S(1)}, f32[3,256,128]{2,1,0:T(8,128)S(1)}, f32[256,128]{1,0:T(8,128)S(1)}) custom-call(f32[3,256,128]{2,1,0:T(8,128)} %bitcast.12, f32[3,256,128]{2,1,0:T(8,128)} %bitcast.13, f32[3,256,128]{2,1,0:T(8,128)} %bitcast.14, f32[3,256,128]{2,1,0:T(8,128)} %bitcast.15, f32[256,128]{1,0:T(8,128)} %bitcast.16, ...), custom_call_target="tpu_custom_call" | custom-call | tf_op jit(solution)/shard_map/pallas_call | solution.py:595
  50.5 0.9 %shard_map.113 = (f32[3,256,128]{2,1,0:T(8,128)}, f32[3,256,128]{2,1,0:T(8,128)}, f32[256,128]{1,0:T(8,128)}) custom-call(f32[3,256,128]{2,1,0:T(8,128)S(1)} %get-tuple-element.9.electric, f32[3,256,128]{2,1,0:T(8,128)S(1)} %get-tuple-element.10.magnetic, f32[256,128]{1,0:T(8,128)S(1)} %get-tuple-element.11.density), custom_call_target="tpu_custom_call" | custom-call | tf_op jit(solution)/shard_map/pallas_call | solution.py:648

commit v4 on v3

--- a/solution.py
+++ b/solution.py
@@ -49,6 +49,7 @@
     v_forward,
     v_mask,
     v_radius,
+    partner,
     efield,
     hfield,
     polar,
@@ -115,6 +116,17 @@
 
     mirror = (nx - 1 - gx, gy)
 
+    barrier = pltpu.get_barrier_semaphore()
+    greeted = jnp.int32(1)
+    for side in SIDES:
+        greeted = greeted + has[side].astype(jnp.int32)
+
+        @pl.when(has[side])
+        def _():
+            pl.semaphore_signal(barrier, inc=1, device_id=device(*side), device_id_type=MESH)
+
+    pl.semaphore_signal(barrier, inc=1, device_id=mirror, device_id_type=MESH)
+
     loads = [
         pltpu.make_async_copy(src, dst, in_sems.at[k])
         for k, (src, dst) in enumerate(
@@ -127,22 +139,12 @@
                 (forward_in, v_forward),
                 (mask_in, v_mask),
                 (radius_in, v_radius),
+                (partner_in, partner),
             ]
         )
     ]
     for load in loads:
         load.start()
-
-    barrier = pltpu.get_barrier_semaphore()
-    greeted = jnp.int32(1)
-    for side in SIDES:
-        greeted = greeted + has[side].astype(jnp.int32)
-
-        @pl.when(has[side])
-        def _():
-            pl.semaphore_signal(barrier, inc=1, device_id=device(*side), device_id_type=MESH)
-
-    pl.semaphore_signal(barrier, inc=1, device_id=mirror, device_id_type=MESH)
 
     lane = lax.broadcasted_iota(jnp.int32, (rows_x, 128), 1)
 
@@ -268,7 +270,7 @@
             weight_radius[y] = jnp.broadcast_to(radii[:, y : y + 1], (rows_x, 128))
 
         filtered_sum(covered, lambda y, total: inv_denom.__setitem__(y, 1.0 / total))
-        for load in loads[2:7]:
+        for load in loads[2:7] + loads[8:]:
             load.wait()
 
     def column_of(ref, x, first):
@@ -291,20 +293,12 @@
             )
 
         return [
+            ((0, -1), copy(2, efield.at[s, 0:2, own(0), :], ye_recv.at[s], (0, -1))),
+            ((0, 1), copy(3, yh_send.at[s], yh_recv.at[s], (0, 1))),
+            ((1, -1), copy(5, efield.at[s, 0, edge(0, rows_x), :], d2_recv.at[s], (1, -1))),
             ((-1, 0), copy(0, xe_send.at[s], xe_recv.at[s], (-1, 0))),
             ((1, 0), copy(1, xh_send.at[s], xh_recv.at[s], (1, 0))),
-            ((0, -1), copy(2, efield.at[s, 0:2, own(0), :], ye_recv.at[s], (0, -1))),
-            ((0, 1), copy(3, yh_send.at[s], yh_recv.at[s], (0, 1))),
             ((-1, 1), copy(4, xe_send.at[s, 1], d1_recv.at[s], (-1, 1))),
-            (
-                (1, -1),
-                copy(
-                    5,
-                    efield.at[s, 0, edge(0, rows_x), :],
-                    d2_recv.at[s],
-                    (1, -1),
-                ),
-            ),
         ]
 
     def start(pairs):
@@ -406,22 +400,45 @@
     flips += [flip(17, ends_send, ends_recv)]
     ends = (0, 1, rows_x - 2, rows_x - 1)
 
-    pending = []
-    for s in range(STEPS):
-
-        def curl_e(y, s=s):
-            curled(s, y)
-
-        over_rows(curl_e)
+    def whole(s, y):
+        hs, news, total = advanced(s, y)
+        for c in range(3):
+            if s + 1 < STEPS:
+                efield[s + 1, c, own(y), :] = news[c]
+            else:
+                o_electric[ORDER[c], pl.ds(y, rows_x, stride=rows_y), :] = news[c]
+                o_magnetic[ORDER[c], pl.ds(y, rows_x, stride=rows_y), :] = hs[c]
+        if s > 0:
+            total = gradient[column(y), :] + total
+        gradient[column(y), :] = total
+
+    def faces_y(s):
+        for k in range(2):
+            yh_send[s, k] = hfield[s, k, own(rows_y), :]
+
+    def faces_x(s):
         for k in range(2):
             xe_send[s, k] = column_of(efield.at[s, 1 + k], 0, 0)[...]
             xh_send[s, k] = column_of(hfield.at[s, 1 + k], rows_x - 1, 1)[...]
-            yh_send[s, k] = hfield[s, k, own(rows_y), :]
-
+
+    pending = []
+    for s in range(STEPS):
+
+        pairs = copies(s)
         if s == 0:
+            over_rows(lambda y: curled(0, y))
+            faces_y(s)
+            faces_x(s)
             pl.semaphore_wait(barrier, greeted)
-        pairs = copies(s)
-        start(pairs)
+            start(pairs)
+        else:
+            curled(s, rows_y - 1)
+            faces_y(s)
+            start(pairs[:3])
+            over_rows(lambda y, s=s: whole(s - 1, y), rows_y - 1, 1)
+            over_rows(lambda y, s=s: curled(s, y), rows_y - 1)
+            faces_x(s)
+            start(pairs[3:])
         if s == 0:
             settle()
             over_rows(
@@ -460,24 +477,14 @@
         column_of(hfield.at[s, 1], -1, 1)[...] = xh_recv[s, 0] - behind_mask_x * xe_send[s, 1] + COURANT * extra
         column_of(hfield.at[s, 2], -1, 1)[...] = xh_recv[s, 1] + behind_mask_x * xe_send[s, 0]
 
-        def curl_h(y, s=s):
-            hs, news, total = advanced(s, y)
-            for c in range(3):
-                if s + 1 < STEPS:
-                    efield[s + 1, c, own(y), :] = news[c]
-                else:
-                    o_electric[ORDER[c], pl.ds(y, rows_x, stride=rows_y), :] = news[c]
-                    o_magnetic[ORDER[c], pl.ds(y, rows_x, stride=rows_y), :] = hs[c]
-            if s > 0:
-                total = gradient[column(y), :] + total
-            gradient[column(y), :] = total
-
-        over_rows(curl_h)
-
+        over_rows(lambda k, s=s: whole(s, k * (rows_y - 1)), 2)
+
+    for copy in flips[3:5]:
+        copy.start()
+    over_rows(lambda y: whole(STEPS - 1, y), rows_y - 1, 1)
     for k, x in enumerate(ends):
         ends_send[k] = gradient[pl.ds(x, rows_y, stride=rows_x), :]
-    for copy in flips[3:]:
-        copy.start()
+    flips[5].start()
     for copy in flips:
         copy.wait_recv()
 
@@ -496,7 +503,7 @@
     over_rows(turn, rows_x)
 
     def update(y):
-        mirrored = g_flip[pl.ds(partner_in[y], rows_x, stride=rows_y), :]
+        mirrored = g_flip[pl.ds(partner[y], rows_x, stride=rows_y), :]
         symmetric = 0.5 * (gradient[column(y), :] + mirrored)
         design = native(v_mask, y).astype(jnp.float32)
         updated[own(y + WIDTH), :] = native(v_density, y) - UPDATE_STEP * design * symmetric
@@ -577,7 +584,7 @@
         return pltpu.VMEM(shape, dtype)
 
     any_spec = pl.BlockSpec(memory_space=pl.ANY)
-    electric, magnetic, polar, rate, density, forward, mask, partner, radius = args
+    electric, magnetic, polar, rate, density, forward, mask, partners, radius = args
     operands = (
         electric.reshape(3, cells, depth),
         magnetic.reshape(3, cells, depth),
@@ -586,10 +593,10 @@
         density.reshape(cells, depth),
         forward.reshape(3 * STEPS, cells, depth),
         mask.reshape(cells, depth),
-        partner,
+        partners,
         radius.T,
     )
-    in_specs = [any_spec] * 7 + [pl.BlockSpec(memory_space=pltpu.SMEM), any_spec]
+    in_specs = [any_spec] * 9
     shapes = ((3, cells, depth), (3, cells, depth), (cells, depth))
     vmem_spec = pl.BlockSpec(memory_space=pltpu.VMEM)
     held = pl.pallas_call(
@@ -606,6 +613,7 @@
             vmem(3 * STEPS, cells, depth),
             vmem(cells, depth, dtype=jnp.int32),
             vmem(rows_y, rows_x, dtype=jnp.int32),
+            pltpu.SMEM((rows_y,), jnp.int32),
             vmem(STEPS, 3, (rows_y + 1) * slab, depth),
             vmem(STEPS, 3, (rows_y + 1) * slab, depth),
             vmem(3, rows_y, rows_x, depth),
@@ -639,7 +647,7 @@
             vmem(2, WIDTH, rows_x, depth),
             vmem(2, WIDTH, rows_x, depth),
             vmem(2, 2, WIDTH, EDGE, depth),
-            pltpu.SemaphoreType.DMA((8,)),
+            pltpu.SemaphoreType.DMA((9,)),
             pltpu.SemaphoreType.DMA((26,)),
             pltpu.SemaphoreType.DMA((26,)),
         ],

time: 52 us -> 52.7 us (1.013)
  Pallas kernels: 50.8 us -> 51.9 us
    pallas_call x1, Pallas kernels: 49.8 us -> 51 us  [local(): pl.pallas_call(functools.partial(kernel, nx, ny), out_shape=tuple((pltpu....]
where the time goes in v4:
time: 52.7 us; the launch traced here: 52.6 us
  Pallas kernels  51.9 us (98%)
  between operations  0.64 us (1%)
    pallas_call x1, Pallas kernels, local(): pl.pallas_call(functools.partial(kernel, nx, ny), out_shape=tuple((pltpu....  51 us

profile of v4, /device:TPU:57, one launch (start us, length us, event | category | flops | bytes accessed | tf_op | source)
XLA Modules:
  0.0 52.6 jit_solution(2192348504025387826)
XLA Ops:
  0.6 51.0 %shard_map.112 = (f32[3,256,128]{2,1,0:T(8,128)S(1)}, f32[3,256,128]{2,1,0:T(8,128)S(1)}, f32[256,128]{1,0:T(8,128)S(1)}) custom-call(f32[3,256,128]{2,1,0:T(8,128)} %bitcast.12, f32[3,256,128]{2,1,0:T(8,128)} %bitcast.13, f32[3,256,128]{2,1,0:T(8,128)} %bitcast.14, f32[3,256,128]{2,1,0:T(8,128)} %bitcast.15, f32[256,128]{1,0:T(8,128)} %bitcast.16, ...), custom_call_target="tpu_custom_call" | custom-call | tf_op jit(solution)/shard_map/pallas_call | solution.py:602
  51.6 0.9 %shard_map.113 = (f32[3,256,128]{2,1,0:T(8,128)}, f32[3,256,128]{2,1,0:T(8,128)}, f32[256,128]{1,0:T(8,128)}) custom-call(f32[3,256,128]{2,1,0:T(8,128)S(1)} %get-tuple-element.9.electric, f32[3,256,128]{2,1,0:T(8,128)S(1)} %get-tuple-element.10.magnetic, f32[256,128]{1,0:T(8,128)S(1)} %get-tuple-element.11.density), custom_call_target="tpu_custom_call" | custom-call | tf_op jit(solution)/shard_map/pallas_call | solution.py:656

commit v5 on v4

--- a/solution.py
+++ b/solution.py
@@ -61,6 +61,7 @@
     g_send,
     g_recv,
     g_turn,
+    g_near,
     g_flip,
     ends_send,
     ends_recv,
@@ -117,15 +118,15 @@
     mirror = (nx - 1 - gx, gy)
 
     barrier = pltpu.get_barrier_semaphore()
+    pl.semaphore_signal(barrier, inc=1, device_id=mirror, device_id_type=MESH)
     greeted = jnp.int32(1)
-    for side in SIDES:
+    for side in sorted(SIDES, key=lambda p: (abs(p[0]), -abs(p[1]))):
         greeted = greeted + has[side].astype(jnp.int32)
 
         @pl.when(has[side])
         def _():
             pl.semaphore_signal(barrier, inc=1, device_id=device(*side), device_id_type=MESH)
 
-    pl.semaphore_signal(barrier, inc=1, device_id=mirror, device_id_type=MESH)
 
     loads = [
         pltpu.make_async_copy(src, dst, in_sems.at[k])
@@ -143,8 +144,8 @@
             ]
         )
     ]
-    for load in loads:
-        load.start()
+    loads[0].start()
+    loads[1].start()
 
     lane = lax.broadcasted_iota(jnp.int32, (rows_x, 128), 1)
 
@@ -176,6 +177,8 @@
         return ref[pl.ds(y, rows_x, stride=rows_y), :]
 
     loads[0].wait()
+    for load in loads[2:]:
+        load.start()
 
     def stage(y):
         for c in range(3):
@@ -262,7 +265,7 @@
 
                 @pl.when(jnp.logical_not(has[2 * k - 1, 2 * j - 1]))
                 def _():
-                    cf_recv[k, j] = jnp.zeros((WIDTH, EDGE, 128), jnp.float32)
+                    cf_recv[k, j] = jnp.zeros((WIDTH, WIDTH, 128), jnp.float32)
 
         loads[7].wait()
         radii = v_radius[...].astype(jnp.float32).T
@@ -270,8 +273,6 @@
             weight_radius[y] = jnp.broadcast_to(radii[:, y : y + 1], (rows_x, 128))
 
         filtered_sum(covered, lambda y, total: inv_denom.__setitem__(y, 1.0 / total))
-        for load in loads[2:7] + loads[8:]:
-            load.wait()
 
     def column_of(ref, x, first):
         return ref.at[pl.ds(first * slab + EDGE + x, rows_y, stride=slab), :]
@@ -395,10 +396,10 @@
 
     inner = pl.ds(2 * rows_x, (rows_y - 4) * rows_x)
     flips = [flip(12, g_send.at[inner, :], g_recv.at[inner, :])]
-    flips += [flip(13 + k, g_send.at[column(y), :], g_recv.at[column(y), :]) for k, y in enumerate((1, rows_y - 2))]
+    flips += [flip(13 + k, g_near.at[column(y), :], g_recv.at[column(y), :]) for k, y in enumerate((1, rows_y - 2))]
     flips += [flip(15 + k, gradient.at[column(y), :], g_recv.at[column(y), :]) for k, y in enumerate((0, rows_y - 1))]
-    flips += [flip(17, ends_send, ends_recv)]
-    ends = (0, 1, rows_x - 2, rows_x - 1)
+    flips += [flip(17 + 9 * k, ends_send.at[pl.ds(2 * (1 - k), 2)], ends_recv.at[pl.ds(2 * (1 - k), 2)]) for k in range(2)]
+    ends = (1, rows_x - 2, 0, rows_x - 1)
 
     def whole(s, y):
         hs, news, total = advanced(s, y)
@@ -420,6 +421,18 @@
         for k in range(2):
             xe_send[s, k] = column_of(efield.at[s, 1 + k], 0, 0)[...]
             xh_send[s, k] = column_of(hfield.at[s, 1 + k], rows_x - 1, 1)[...]
+
+    def drive(s, y):
+        driven_by(s, y, [efield[s, c, own(y), :] for c in range(3)])
+
+    def prepare():
+        for load in loads[2:7] + loads[8:]:
+            load.wait()
+        over_rows(
+            lambda y: inv_eps.__setitem__(y, 1.0 / (1.0 + (EPS_MATERIAL - 1.0) * native(v_density, y)))
+        )
+        over_rows(lambda y: drive(0, y))
+        inner_rows()
 
     pending = []
     for s in range(STEPS):
@@ -440,25 +453,20 @@
             faces_x(s)
             start(pairs[3:])
         if s == 0:
+            prepare()
+            flips[0].start()
             settle()
-            over_rows(
-                lambda y: inv_eps.__setitem__(
-                    y, 1.0 / (1.0 + (EPS_MATERIAL - 1.0) * native(v_density, y))
-                )
-            )
-
-        def drive(y, s=s):
-            driven_by(s, y, [efield[s, c, own(y), :] for c in range(3)])
-
-        over_rows(drive)
-        if s == 0:
-            inner_rows()
-            flips[0].start()
         else:
-            for y in (1, rows_y - 2):
-                g_send[column(y), :] = gradient[column(y), :] + advanced(s, y)[2]
-            flips[1].start()
-            flips[2].start()
+            over_rows(lambda y, s=s: drive(s, y))
+
+            def near(y):
+                g_near[column(y), :] = gradient[column(y), :] + advanced(STEPS - 1, y)[2]
+
+            over_rows(near, rows_y - 1, 1)
+            for k, x in enumerate((1, rows_x - 2)):
+                ends_send[k] = g_near[pl.ds(x, rows_y, stride=rows_x), :]
+            for copy in flips[1:3] + flips[6:]:
+                copy.start()
         arrive(pairs)
         pending += pairs
 
@@ -482,18 +490,20 @@
     for copy in flips[3:5]:
         copy.start()
     over_rows(lambda y: whole(STEPS - 1, y), rows_y - 1, 1)
-    for k, x in enumerate(ends):
-        ends_send[k] = gradient[pl.ds(x, rows_y, stride=rows_x), :]
+    for k, x in enumerate((0, rows_x - 1)):
+        ends_send[2 + k] = gradient[pl.ds(x, rows_y, stride=rows_x), :]
     flips[5].start()
     for copy in flips:
         copy.wait_recv()
 
-    def spread(y):
-        g_turn[pl.ds(y, rows_x, stride=rows_y), :] = g_recv[column(y), :]
-
-    over_rows(spread)
+    def spread(ref, y):
+        g_turn[pl.ds(y, rows_x, stride=rows_y), :] = ref[column(y), :]
+
+    over_rows(lambda y: spread(g_recv, y))
     for k, x in enumerate(ends):
         g_turn[pl.ds(x * rows_y, rows_y), :] = ends_recv[k]
+    for y in (0, rows_y - 1):
+        spread(g_recv, y)
 
     def turn(x):
         g_flip[pl.ds(pl.multiple_of(x * rows_y, rows_y), rows_y), :] = g_turn[
@@ -523,7 +533,7 @@
         elif i == 0:
             src, dst = yf_send.at[(j + 1) // 2], yf_recv.at[(1 - j) // 2]
         else:
-            xs = slice(0, EDGE) if i < 0 else slice(rows_x - EDGE, rows_x)
+            xs = slice(0, WIDTH) if i < 0 else slice(rows_x - WIDTH, rows_x)
             src, dst = yf_send.at[(j + 1) // 2, :, xs, :], cf_recv.at[(1 - i) // 2, (1 - j) // 2]
         halos.append(
             (
@@ -546,8 +556,8 @@
         for j in range(2):
             y = r + j * (WIDTH + rows_y)
             updated[own(y), :] = yf_recv[j, r]
-            updated[edge(y, 0), :] = cf_recv[0, j, r]
-            updated[edge(y, EDGE + rows_x), :] = cf_recv[1, j, r]
+            updated[rows(y, EDGE - WIDTH, WIDTH), :] = cf_recv[0, j, r]
+            updated[rows(y, EDGE + rows_x, WIDTH), :] = cf_recv[1, j, r]
 
     top = math.tanh(SHARPNESS * THRESHOLD)
     bottom = top + math.tanh(SHARPNESS * (1.0 - THRESHOLD))
@@ -567,6 +577,7 @@
 
 def write_out(electric, magnetic, density, electric_out, magnetic_out, density_out, sems):
     pairs = ((electric, electric_out), (magnetic, magnetic_out), (density, density_out))
+    pairs = [(src.at[c], dst.at[c]) for src, dst in pairs[:2] for c in range(3)] + [pairs[2]]
     stores = [pltpu.make_async_copy(src, dst, sems.at[k]) for k, (src, dst) in enumerate(pairs)]
     for store in stores:
         store.start()
@@ -626,6 +637,7 @@
             vmem(cells, depth),
             vmem(cells, depth),
             vmem(cells, depth),
+            vmem(cells, depth),
             vmem(4, rows_y, depth),
             vmem(4, rows_y, depth),
             vmem((rows_y + 2 * WIDTH) * slab, depth),
@@ -646,10 +658,10 @@
             vmem(2, WIDTH, rows_y, depth),
             vmem(2, WIDTH, rows_x, depth),
             vmem(2, WIDTH, rows_x, depth),
-            vmem(2, 2, WIDTH, EDGE, depth),
+            vmem(2, 2, WIDTH, WIDTH, depth),
             pltpu.SemaphoreType.DMA((9,)),
-            pltpu.SemaphoreType.DMA((26,)),
-            pltpu.SemaphoreType.DMA((26,)),
+            pltpu.SemaphoreType.DMA((27,)),
+            pltpu.SemaphoreType.DMA((27,)),
         ],
         compiler_params=pltpu.CompilerParams(collective_id=0, has_side_effects=True),
     )(*operands)
@@ -658,7 +670,7 @@
         out_shape=tuple(jax.ShapeDtypeStruct(shape, f32) for shape in shapes),
         in_specs=[vmem_spec] * 3,
         out_specs=(any_spec,) * 3,
-        scratch_shapes=[pltpu.SemaphoreType.DMA((3,))],
+        scratch_shapes=[pltpu.SemaphoreType.DMA((7,))],
     )(*[pltpu.with_memory_space_constraint(a, pltpu.VMEM) for a in held])
     return (
         outs[0].reshape(electric.shape),

time: 52.7 us -> 50.6 us (0.960)
  the two profiles are of different devices: /device:TPU:57 before, /device:TPU:127 now
where the time goes in v5:
time: 50.6 us; the launch traced here: 50.4 us
  Pallas kernels  49.8 us (98%)
  between operations  0.64 us (1%)
    pallas_call x1, Pallas kernels, local(): pl.pallas_call(functools.partial(kernel, nx, ny), out_shape=tuple((pltpu....  48.8 us

profile of v5, /device:TPU:127, one launch (start us, length us, event | category | flops | bytes accessed | tf_op | source)
XLA Modules:
  0.0 50.4 jit_solution(13502936025612826342)
XLA Ops:
  0.6 48.8 %shard_map.112 = (f32[3,256,128]{2,1,0:T(8,128)S(1)}, f32[3,256,128]{2,1,0:T(8,128)S(1)}, f32[256,128]{1,0:T(8,128)S(1)}) custom-call(f32[3,256,128]{2,1,0:T(8,128)} %bitcast.12, f32[3,256,128]{2,1,0:T(8,128)} %bitcast.13, f32[3,256,128]{2,1,0:T(8,128)} %bitcast.14, f32[3,256,128]{2,1,0:T(8,128)} %bitcast.15, f32[256,128]{1,0:T(8,128)} %bitcast.16, ...), custom_call_target="tpu_custom_call" | custom-call | tf_op jit(solution)/shard_map/pallas_call | solution.py:613
  49.4 1.0 %shard_map.113 = (f32[3,256,128]{2,1,0:T(8,128)}, f32[3,256,128]{2,1,0:T(8,128)}, f32[256,128]{1,0:T(8,128)}) custom-call(f32[3,256,128]{2,1,0:T(8,128)S(1)} %get-tuple-element.9.electric, f32[3,256,128]{2,1,0:T(8,128)S(1)} %get-tuple-element.10.magnetic, f32[256,128]{1,0:T(8,128)S(1)} %get-tuple-element.11.density), custom_call_target="tpu_custom_call" | custom-call | tf_op jit(solution)/shard_map/pallas_call | solution.py:668

commit v6 on v5

--- a/solution.py
+++ b/solution.py
@@ -156,11 +156,14 @@
         return jnp.where(lane > 0, pltpu.roll(v, 1, 1), 0.0)
 
     def over_rows(body, stop=rows_y, start=0):
-        def step(y, carry):
-            body(y)
+        group = math.gcd(4, stop - start)
+
+        def step(i, carry):
+            for k in range(group):
+                body(start + i * group + k)
             return carry
 
-        lax.fori_loop(start, stop, step, 0)
+        lax.fori_loop(0, (stop - start) // group, step, 0)
 
     zeros_slab = jnp.zeros((rows_x, 128), jnp.float32)
     zeros_edge = jnp.zeros((EDGE, 128), jnp.float32)

time: 50.6 us -> 50.3 us (level)
  the two profiles are of different devices: /device:TPU:127 before, /device:TPU:111 now
where the time goes in v6:
time: 50.3 us; the launch traced here: 50.2 us
  Pallas kernels  49.5 us (98%)
  between operations  0.64 us (1%)
    pallas_call x1, Pallas kernels, local(): pl.pallas_call(functools.partial(kernel, nx, ny), out_shape=tuple((pltpu....  48.5 us

profile of v6, /device:TPU:111, one launch (start us, length us, event | category | flops | bytes accessed | tf_op | source)
XLA Modules:
  0.0 50.2 jit_solution(5176646850706448349)
XLA Ops:
  0.6 48.5 %shard_map.112 = (f32[3,256,128]{2,1,0:T(8,128)S(1)}, f32[3,256,128]{2,1,0:T(8,128)S(1)}, f32[256,128]{1,0:T(8,128)S(1)}) custom-call(f32[3,256,128]{2,1,0:T(8,128)} %bitcast.12, f32[3,256,128]{2,1,0:T(8,128)} %bitcast.13, f32[3,256,128]{2,1,0:T(8,128)} %bitcast.14, f32[3,256,128]{2,1,0:T(8,128)} %bitcast.15, f32[256,128]{1,0:T(8,128)} %bitcast.16, ...), custom_call_target="tpu_custom_call" | custom-call | tf_op jit(solution)/shard_map/pallas_call | solution.py:616
  49.2 1.0 %shard_map.113 = (f32[3,256,128]{2,1,0:T(8,128)}, f32[3,256,128]{2,1,0:T(8,128)}, f32[256,128]{1,0:T(8,128)}) custom-call(f32[3,256,128]{2,1,0:T(8,128)S(1)} %get-tuple-element.9.electric, f32[3,256,128]{2,1,0:T(8,128)S(1)} %get-tuple-element.10.magnetic, f32[256,128]{1,0:T(8,128)S(1)} %get-tuple-element.11.density), custom_call_target="tpu_custom_call" | custom-call | tf_op jit(solution)/shard_map/pallas_call | solution.py:671

commit v7 on v6

--- a/solution.py
+++ b/solution.py
@@ -496,17 +496,27 @@
     for k, x in enumerate((0, rows_x - 1)):
         ends_send[2 + k] = gradient[pl.ds(x, rows_y, stride=rows_x), :]
     flips[5].start()
-    for copy in flips:
+    def weigh(y):
+        step = (0.5 * UPDATE_STEP) * native(v_mask, y).astype(jnp.float32)
+        kept[0, y] = native(v_density, y) - step * gradient[column(y), :]
+        kept[1, y] = step
+
+    over_rows(weigh)
+
+    def spread(y):
+        g_turn[pl.ds(y, rows_x, stride=rows_y), :] = g_recv[column(y), :]
+
+    for copy in flips[:3] + flips[6:]:
         copy.wait_recv()
-
-    def spread(ref, y):
-        g_turn[pl.ds(y, rows_x, stride=rows_y), :] = ref[column(y), :]
-
-    over_rows(lambda y: spread(g_recv, y))
-    for k, x in enumerate(ends):
-        g_turn[pl.ds(x * rows_y, rows_y), :] = ends_recv[k]
+    over_rows(spread, rows_y - 1, 1)
+    for k in (0, 1):
+        g_turn[pl.ds(ends[k] * rows_y, rows_y), :] = ends_recv[k]
+    for copy in flips[3:6]:
+        copy.wait_recv()
+    for k in (2, 3):
+        g_turn[pl.ds(ends[k] * rows_y, rows_y), :] = ends_recv[k]
     for y in (0, rows_y - 1):
-        spread(g_recv, y)
+        spread(y)
 
     def turn(x):
         g_flip[pl.ds(pl.multiple_of(x * rows_y, rows_y), rows_y), :] = g_turn[
@@ -517,9 +527,7 @@
 
     def update(y):
         mirrored = g_flip[pl.ds(partner[y], rows_x, stride=rows_y), :]
-        symmetric = 0.5 * (gradient[column(y), :] + mirrored)
-        design = native(v_mask, y).astype(jnp.float32)
-        updated[own(y + WIDTH), :] = native(v_density, y) - UPDATE_STEP * design * symmetric
+        updated[own(y + WIDTH), :] = kept[0, y] - kept[1, y] * mirrored
 
     over_rows(update)
 

time: 50.3 us -> 50.2 us (level)
  no operation moved by 1% of the time
where the time goes in v7:
time: 50.2 us; the launch traced here: 50.1 us
  Pallas kernels  49.4 us (98%)
  between operations  0.64 us (1%)
    pallas_call x1, Pallas kernels, local(): pl.pallas_call(functools.partial(kernel, nx, ny), out_shape=tuple((pltpu....  48.4 us

profile of v7, /device:TPU:111, one launch (start us, length us, event | category | flops | bytes accessed | tf_op | source)
XLA Modules:
  0.0 50.1 jit_solution(16024961037711197896)
XLA Ops:
  0.6 48.4 %shard_map.112 = (f32[3,256,128]{2,1,0:T(8,128)S(1)}, f32[3,256,128]{2,1,0:T(8,128)S(1)}, f32[256,128]{1,0:T(8,128)S(1)}) custom-call(f32[3,256,128]{2,1,0:T(8,128)} %bitcast.12, f32[3,256,128]{2,1,0:T(8,128)} %bitcast.13, f32[3,256,128]{2,1,0:T(8,128)} %bitcast.14, f32[3,256,128]{2,1,0:T(8,128)} %bitcast.15, f32[256,128]{1,0:T(8,128)} %bitcast.16, ...), custom_call_target="tpu_custom_call" | custom-call | tf_op jit(solution)/shard_map/pallas_call | solution.py:624
  49.1 1.0 %shard_map.113 = (f32[3,256,128]{2,1,0:T(8,128)}, f32[3,256,128]{2,1,0:T(8,128)}, f32[256,128]{1,0:T(8,128)}) custom-call(f32[3,256,128]{2,1,0:T(8,128)S(1)} %get-tuple-element.9.electric, f32[3,256,128]{2,1,0:T(8,128)S(1)} %get-tuple-element.10.magnetic, f32[256,128]{1,0:T(8,128)S(1)} %get-tuple-element.11.density), custom_call_target="tpu_custom_call" | custom-call | tf_op jit(solution)/shard_map/pallas_call | solution.py:679
